TPU v7x, 32 devices: a whole 2x2x4 slice. The times are simulated.
32 devices in a mesh: batch: 16 (over z, y, core), head: 2 (over x).
Axes of the slice: x: 2, y: 2, z: 4, core: 2. Of those that a mesh axis runs over, the one named last changes fastest.
Arguments:
- tokens: bfloat16 [14336, 1024], P('batch', 'head'), may hold values from -6 to 6
- ln_gain: float32 [1024], replicated, may hold values from 0.5 to 1.5
- w_qkv: bfloat16 [1024, 3072], P(None, 'head'), may hold values from -0.1875 to 0.1875
- qk_gain: float32 [2, 64], replicated, may hold values from 1 to 1.7
- w_out: bfloat16 [1024, 1024], P('head'), may hold values from -1 to 1
- w_up: bfloat16 [1024, 4096], P(None, 'head'), may hold values from -0.1875 to 0.1875
- b_up: float32 [4096], P('head'), may hold values from -3 to 3
- w_down: bfloat16 [4096, 1024], P('head'), may hold values from -0.09375 to 0.09375
- b_out: float32 [1024], P('head'), may hold values from -3 to 3
- cotangent: bfloat16 [14336, 1024], P('batch', 'head'), may hold values from -6 to 6
- slot_image: int32 [64], P('batch'), may hold values from 0 to 3, as said below
- token_valid: int32 [14336], P('batch'), may hold values from 0 to 1, as said below
Outputs:
- output: bfloat16 [14336, 1024], P('batch', 'head')
- grad_tokens: bfloat16 [14336, 1024], P('batch', 'head')
- grad_ln_gain: float32 [1024], P('head')
- grad_w_qkv: float32 [1024, 3072], P(None, 'head')
- grad_qk_gain: float32 [2, 64], replicated
- grad_w_out: float32 [1024, 1024], P('head')
- grad_w_up: float32 [1024, 4096], P(None, 'head')
- grad_b_up: float32 [4096], P('head')
- grad_w_down: float32 [4096, 1024], P('head')
- grad_b_out: float32 [1024], P('head')
Inputs may be any that keep to these rules, and one draw needn't show every extreme that they name: `slot_image`: within each group of 4 slots the image numbers start at 0, never fall, and rise by one from slot to slot, except that a long image takes the first 3 slots of some groups (at least one group in every draw); every other image takes one slot. `token_valid`: in each slot the valid rows come first; a long image has all of its 672 rows valid; a one-slot image has 112 to 196 valid rows, and the first one-slot image of every group has exactly 196.
All inputs are finite; a program needn't handle non-finite values.
Results may differ from a plain program's by a relative error of at most 0.012.
Values may be sent and summed in bfloat16 or wider, within the bound.
No kernel may reach another device: no remote copies, remote signals or barrier semaphores. Data moves between devices by JAX's collectives and lax.ppermute only.
A program may use at most 192 MiB of HBM per device.

v0:
```python
import jax
import jax.numpy as jnp
from jax import lax
from jax.sharding import PartitionSpec as P

HD = 64


EPSILON = 1e-06
NEGATIVE = -1e30


def row_norm(values):
    center = jnp.mean(values, axis=-1, keepdims=True)
    shifted = values - center
    spread = jnp.mean(shifted * shifted, axis=-1, keepdims=True)
    scaled = lax.rsqrt(spread + EPSILON)
    return (shifted * scaled, scaled)


def head_norm(values, gain):
    normal_part, scaled = row_norm(values)
    return normal_part * gain


def contract(left, right, left_dim, right_dim):
    return lax.dot_general(
        left, right, (((left_dim,), (right_dim,)), ((), ())), preferred_element_type=jnp.float32
    )


def prepare(gathered, ln_gain, w_qkv, qk_gain, w_up, b_up):
    row_count = gathered.shape[0]
    x_hat, scaled = row_norm(gathered.astype(jnp.float32))
    normed = (x_hat * ln_gain).astype(jnp.bfloat16)
    joined = jnp.dot(normed, w_qkv, preferred_element_type=jnp.float32).reshape(
        row_count, -1, 3, HD
    )
    query_raw = joined[:, :, 0]
    key_raw = joined[:, :, 1]
    query_norm = head_norm(query_raw, qk_gain[0]).astype(jnp.bfloat16)
    key_norm = head_norm(key_raw, qk_gain[1]).astype(jnp.bfloat16)
    value_low = joined[:, :, 2].astype(jnp.bfloat16)
    pre_gate = jnp.dot(normed, w_up, preferred_element_type=jnp.float32) + b_up
    hidden = jax.nn.gelu(pre_gate, approximate=False).astype(jnp.bfloat16)
    return (
        x_hat,
        scaled,
        normed,
        query_raw,
        key_raw,
        query_norm,
        key_norm,
        value_low,
        pre_gate,
        hidden,
    )


def key_span(slot_image, block_index):
    first_image = slot_image[4 * block_index]
    last_image = slot_image[4 * block_index + 3]
    first_block = jnp.sum(slot_image < first_image) // 4
    stop_block = (jnp.sum(slot_image <= last_image) - 1) // 4 + 1
    return (first_block, stop_block)


def block_scores(
    query_block, query_image, key_norm, token_image, usable_key, key_block, block_rows
):
    key_start = key_block * block_rows
    scores = jnp.einsum(
        "qhe,khe->hqk", query_block, key_norm, preferred_element_type=jnp.float32
    ) * float(HD) ** (-0.5)
    key_image = lax.dynamic_slice_in_dim(token_image, key_start, block_rows, 0)
    allowed = (query_image[:, None] == key_image[None, :]) & usable_key[None, :]
    return (scores, allowed[None], key_norm)


def attend(query_norm, key_norm, value_low, token_image, usable_key, slot_image, block_rows):
    row_count, heads_local, head_size = query_norm.shape

    def one_block(block_index):
        row_start = block_index * block_rows
        query_image = lax.dynamic_slice_in_dim(token_image, row_start, block_rows, 0)
        first_block, stop_block = key_span(slot_image, block_index)

        def first_pass(key_block, carry):
            row_peak, row_total = carry
            scores, allowed, key_rows = block_scores(
                query_norm, query_image, key_norm, token_image, usable_key, key_block, block_rows
            )
            masked = jnp.where(allowed, scores, NEGATIVE)
            new_peak = jnp.maximum(row_peak, jnp.max(masked, axis=-1))
            terms = jnp.where(allowed, jnp.exp(masked - new_peak[..., None]), 0.0)
            return (new_peak, row_total * jnp.exp(row_peak - new_peak) + jnp.sum(terms, axis=-1))

        initial = (
            jnp.full((heads_local, block_rows), NEGATIVE, jnp.float32),
            jnp.zeros((heads_local, block_rows), jnp.float32),
        )
        row_peak, row_total = lax.fori_loop(first_block, stop_block, first_pass, initial)
        log_total = row_peak + jnp.log(row_total)

        def second_pass(key_block, running):
            scores, allowed, key_rows = block_scores(
                query_norm, query_image, key_norm, token_image, usable_key, key_block, block_rows
            )
            softmax_low = jnp.where(allowed, jnp.exp(scores - log_total[..., None]), 0.0).astype(
                jnp.bfloat16
            )
            return running + jnp.einsum(
                "hqk,khe->qhe", softmax_low, value_low, preferred_element_type=jnp.float32
            )

        result = lax.fori_loop(
            first_block,
            stop_block,
            second_pass,
            jnp.zeros((block_rows, heads_local, head_size), jnp.float32),
        )
        return (result, log_total)

    results, log_totals = lax.map(one_block, jnp.arange(row_count // block_rows, dtype=jnp.int32))
    attended = results.reshape(row_count, heads_local, head_size)
    log_total = jnp.transpose(log_totals, (1, 0, 2)).reshape(heads_local, row_count)
    return (attended, log_total)


def attend_back(
    query_norm,
    key_norm,
    value_low,
    token_image,
    usable_key,
    slot_image,
    block_rows,
    log_total,
    grad_out,
    row_inner,
):
    row_count, heads_local, head_size = query_norm.shape
    factor = float(HD) ** (-0.5)

    def one_block(block_index, carry):
        grad_query_all, grad_key_all, grad_value_all = carry
        row_start = block_index * block_rows
        query_image = lax.dynamic_slice_in_dim(token_image, row_start, block_rows, 0)
        first_block, stop_block = key_span(slot_image, block_index)

        def inner(key_block, inner_carry):
            grad_query_block, grad_key_run, grad_value_run = inner_carry
            scores, allowed, key_rows = block_scores(
                query_norm, query_image, key_norm, token_image, usable_key, key_block, block_rows
            )
            key_start = key_block * block_rows
            weights = jnp.where(allowed, jnp.exp(scores - log_total[..., None]), 0.0)
            grad_weights = jnp.einsum(
                "qhe,khe->hqk", grad_out, value_low, preferred_element_type=jnp.float32
            )
            grad_scores = (weights * (grad_weights - row_inner[..., None])).astype(jnp.bfloat16)
            grad_query_block = (
                grad_query_block
                + jnp.einsum(
                    "hqk,khe->qhe", grad_scores, key_rows, preferred_element_type=jnp.float32
                )
                * factor
            )
            key_term = (
                jnp.einsum(
                    "hqk,qhe->khe", grad_scores, query_norm, preferred_element_type=jnp.float32
                )
                * factor
            )
            value_term = jnp.einsum(
                "hqk,qhe->khe",
                weights.astype(jnp.bfloat16),
                grad_out,
                preferred_element_type=jnp.float32,
            )
            grad_key_run = lax.dynamic_update_slice_in_dim(
                grad_key_run, grad_key_run + key_term, key_start, 0
            )
            grad_value_run = lax.dynamic_update_slice_in_dim(
                grad_value_run, grad_value_run + value_term, key_start, 0
            )
            return (grad_query_block, grad_key_run, grad_value_run)

        initial = (
            jnp.zeros((block_rows, heads_local, head_size), jnp.float32),
            grad_key_all,
            grad_value_all,
        )
        grad_query_block, grad_key_all, grad_value_all = lax.fori_loop(
            first_block, stop_block, inner, initial
        )
        grad_query_all = grad_query_block
        return (grad_query_all, grad_key_all, grad_value_all)

    empty = jnp.zeros((row_count, heads_local, head_size), jnp.float32)
    return lax.fori_loop(0, row_count // block_rows, one_block, (empty, empty, empty))


def on_device(
    tokens,
    ln_gain,
    w_qkv,
    qk_gain,
    w_out,
    w_up,
    b_up,
    w_down,
    b_out,
    cotangent,
    slot_image,
    token_valid,
):
    row_count, width_local = tokens.shape
    slot_rows = row_count // slot_image.shape[0]
    block_rows = 4 * slot_rows
    token_image = jnp.repeat(slot_image, slot_rows, total_repeat_length=row_count)
    usable_key = token_valid == 1
    gathered = lax.all_gather(tokens, "head", axis=1, tiled=True)
    x_hat, scaled, normed, query_raw, key_raw, query_norm, key_norm, value_low, pre_gate, hidden = (
        prepare(gathered, ln_gain, w_qkv, qk_gain, w_up, b_up)
    )
    attended, log_total = attend(
        query_norm, key_norm, value_low, token_image, usable_key, slot_image, block_rows
    )
    heads_local = query_norm.shape[1]
    attended_low = attended.reshape(row_count, -1).astype(jnp.bfloat16)
    branch_terms = jnp.dot(attended_low, w_out, preferred_element_type=jnp.float32) + jnp.dot(
        hidden, w_down, preferred_element_type=jnp.float32
    )
    summed = lax.psum_scatter(
        branch_terms.astype(jnp.bfloat16), "head", scatter_dimension=1, tiled=True
    ).astype(jnp.float32)
    output = (tokens.astype(jnp.float32) + summed + b_out).astype(jnp.bfloat16)
    regathered = lax.all_gather(tokens, "head", axis=1, tiled=True)
    x_hat, scaled, normed, query_raw, key_raw, query_norm, key_norm, value_low, pre_gate, hidden = (
        prepare(regathered, ln_gain, w_qkv, qk_gain, w_up, b_up)
    )
    full_width = gathered.shape[1]
    piece = lax.all_gather(cotangent, "head", axis=1, tiled=True)
    grad_attended = contract(piece, w_out, 1, 1)
    grad_hidden = contract(piece, w_down, 1, 1)
    grad_wo = contract(attended_low, piece, 0, 0)
    grad_wd = contract(hidden, piece, 0, 0)
    grad_attended, grad_hidden, grad_wo, grad_wd = (grad_attended, grad_hidden, grad_wo, grad_wd)
    grad_out = grad_attended.astype(jnp.bfloat16).reshape(row_count, heads_local, HD)
    row_inner = jnp.transpose(jnp.sum(grad_out.astype(jnp.float32) * attended, axis=-1))
    grad_query, grad_key, grad_value = attend_back(
        query_norm,
        key_norm,
        value_low,
        token_image,
        usable_key,
        slot_image,
        block_rows,
        log_total,
        grad_out,
        row_inner,
    )

    def both_norms(query_in, key_in, gains):
        return (head_norm(query_in, gains[0]), head_norm(key_in, gains[1]))

    unused_pair, norm_back = jax.vjp(both_norms, query_raw, key_raw, qk_gain)
    grad_query_raw, grad_key_raw, grad_qk_gain = norm_back((grad_query, grad_key))
    grad_joined = (
        jnp.stack([grad_query_raw, grad_key_raw, grad_value], axis=2)
        .reshape(row_count, -1)
        .astype(jnp.bfloat16)
    )
    unused_gelu, gelu_back = jax.vjp(lambda z: jax.nn.gelu(z, approximate=False), pre_gate)
    grad_pre = gelu_back(grad_hidden)[0].astype(jnp.bfloat16)
    grad_b_up = jnp.sum(grad_pre.astype(jnp.float32), axis=0)
    grad_wqkv = contract(normed, grad_joined, 0, 0)
    grad_wup = contract(normed, grad_pre, 0, 0)
    grad_norm_part = contract(grad_joined, w_qkv, 1, 1) + contract(grad_pre, w_up, 1, 1)
    grad_normed = lax.psum_scatter(
        grad_norm_part.astype(jnp.bfloat16), "head", scatter_dimension=1, tiled=True
    ).astype(jnp.float32)
    col_start = lax.axis_index("head") * width_local
    x_hat_local = lax.dynamic_slice_in_dim(x_hat, col_start, width_local, 1)
    gain_local = lax.dynamic_slice_in_dim(ln_gain, col_start, width_local, 0)
    grad_hat = grad_normed * gain_local
    first_sum, second_sum, qk_total = lax.psum(
        (jnp.sum(grad_hat, axis=1), jnp.sum(grad_hat * x_hat_local, axis=1), grad_qk_gain), "head"
    )
    grad_tokens = cotangent.astype(jnp.float32) + scaled * (
        grad_hat
        - first_sum[:, None] / full_width
        - x_hat_local * (second_sum[:, None] / full_width)
    )
    grad_ln_local = jnp.sum(grad_normed * x_hat_local, axis=0)
    grad_b_out = jnp.sum(cotangent.astype(jnp.float32), axis=0)
    reduced = lax.psum(
        (grad_ln_local, grad_wqkv, grad_wo, grad_wup, grad_b_up, grad_wd, grad_b_out, qk_total),
        "batch",
    )
    return (
        output,
        grad_tokens.astype(jnp.bfloat16),
        reduced[0],
        reduced[1],
        reduced[7],
        reduced[2],
        reduced[3],
        reduced[4],
        reduced[5],
        reduced[6],
    )


def solution(mesh):
    placed = (
        P("batch", "head"),
        P(),
        P(None, "head"),
        P(),
        P("head", None),
        P(None, "head"),
        P("head"),
        P("head", None),
        P("head"),
        P("batch", "head"),
        P("batch"),
        P("batch"),
    )
    return jax.shard_map(
        on_device,
        mesh=mesh,
        in_specs=placed,
        out_specs=(
            P("batch", "head"),
            P("batch", "head"),
            P("head"),
            P(None, "head"),
            P(),
            P("head", None),
            P(None, "head"),
            P("head"),
            P("head", None),
            P("head"),
        ),
        check_vma=False,
    )
```

profile of v0, /device:TPU:0, one launch (start us, length us, event | category | flops | bytes accessed | tf_op | source)
XLA Modules:
  0.0 807.7 jit_solution(3870349327625631560)
XLA Ops:
  10.1 2.6 fusion.30
  17.4 3.3 select_select_fusion.1
  22.2 20.2 %all-gather.3.cloned.1.call-done = bf16[896,1024]{1,0:T(8,128)(2,1)} async-done(((bf16[896,512]{1,0:T(8,128)(2,1)}), bf16[896,1024]{1,0:T(8,128)(2,1)}) %all-gather.3.cloned.1.call-update) | async-done | bytes 1835024 | tf_op jit(solution)/shard_map/all_gather | solution.py:223
  42.5 1.9 convert_reduce_fusion.1
  44.4 2.1 fusion.12
  46.6 3.8 fusion.39
  53.9 10.3 %fusion.42 = f32[8,896,896]{2,1,0:T(8,128)} fusion(bf16[896,8,64]{0,2,1:T(8,128)(2,1)S(1)} %multiply_convert_fusion.4, bf16[896,8,64]{0,2,1:T(8,128)(2,1)S(1)} %multiply_convert_fusion.3), kind=kOutput, calls=%fused_computation.111 | convolution fusion | flops 822083584 | bytes 27525120 | tf_op jit(solution)/shard_map/while/body/eval_jaxpr/while/body/qhe,khe->hqk/dot_general | solution.py:72
  64.2 30.0 %while.71 = (s32[]{:T(128)}, f32[8,896]{1,0:T(8,128)S(1)}, f32[8,896]{1,0:T(8,128)S(1)}, s32[]{:T(128)}, pred[896]{0:T(1024)(128)(4,1)S(1)}, /*index=5*/bf16[896...) while((s32[]{:T(128)}, f32[8,896]{1,0:T(8,128)S(1)}, ...), condition=%wide.region_11.12_spmd.clone, body=%wide.region_8.11_spmd.clone.sunk | while | flops 875086464 | bytes 56007324 | solution.py:102
  64.5 2.6 select_select_fusion.3
  67.9 14.0 %fusion.86 = (f32[8,896]{1,0:T(8,128)S(1)}, f32[8,896,896]{1,2,0:T(8,128)}) fusion(pred[896,896]{0,1:T(8,128)(4,1)S(1)} %compare_and_fusion.3, bf16[896,8,64]{0,2,1:T(8,128)(2,1)} %get-tuple-element.794, bf16[896,8,64]{0,2,1:T(8,128)(2,1)} %get-tuple-element.795), kind=kOutput, calls=%fused_computation.7.clone.1 | convolution fusion | flops 841344000 | bytes 28356608 | tf_op jit(solution)/shard_map/while/body/eval_jaxpr/while/body/qhe,khe->hqk/dot_general | solution.py:72
  81.9 12.0 %select_reduce_fusion.2 = f32[8,896]{1,0:T(8,128)S(1)} fusion(f32[8,896,896]{1,2,0:T(8,128)} %get-tuple-element.758, f32[8,896]{1,0:T(8,128)S(1)} %max.6, pred[896,896]{0,1:T(8,128)(4,1)S(1)} %compare_and_fusion.3), kind=kLoop, calls=%fused_computation.5.clone.1 | loop fusion | flops 32105472 | bytes 26550272 | tf_op jit(solution)/shard_map/while/body/eval_jaxpr/while/body/reduce_sum | solution.py:96
  94.2 13.1 %fusion.25 = f32[8,896,64]{1,2,0:T(8,128)} fusion(f32[8,896,896]{2,1,0:T(8,128)} %fusion.42, f32[8,896]{1,0:T(8,128)S(1)} %log_add_fusion, pred[896,896]{1,0:T(8,128)(4,1)} %compare_and_fusion.1, f32[896,8,3,64]{0,3,2,1:T(8,128)} %bitcast.109), kind=kOutput, calls=%fused_computation.78 | convolution fusion | flops 847773696 | bytes 29274112 | tf_op jit(solution)/shard_map/while/body/eval_jaxpr/while/body/hqk,khe->qhe/dot_general | solution.py:112
  107.3 3.1 convolution_convert_fusion
  111.4 12.0 %fusion.31 = f32[8,896,64]{1,2,0:T(8,128)} fusion(bf16[896,8,64]{0,2,1:T(8,128)(2,1)S(1)} %bitcast.122, f32[8,896,896]{2,1,0:T(8,128)} %fusion.42, f32[8,896]{1,0:T(8,128)S(1)} %log_add_fusion, pred[896,896]{1,0:T(8,128)(4,1)S(1)} %copy-done.28), kind=kOutput, calls=%fused_computation.103 | convolution fusion | flops 847773696 | bytes 29274112 | tf_op jit(solution)/shard_map/while/body/eval_jaxpr/while/body/hqk,qhe->khe/dot_general | solution.py:175
  123.4 3.4 copy.55
  126.8 3.7 copy.53
  130.5 2.0 broadcast.423.clone
  132.5 5.8 while.69
  132.5 5.3 bitcast_add_fusion.7
  138.3 4.4 multiply_reduce_fusion
  143.9 14.7 %multiply_convert_fusion = bf16[8,896,896]{2,1,0:T(8,128)(2,1)S(1)} fusion(f32[8,896,896]{2,1,0:T(8,128)} %fusion.42, f32[8,896]{1,0:T(8,128)S(1)} %copy.56, f32[8,896]{1,0:T(8,128)S(1)} %log_add_fusion, pred[896,896]{1,0:T(8,128)(4,1)} %compare_and_fusion.1, bf16[896,8,64]{0,2,1:T(8,128)(2,1)} %bitcast.124, f32[896,8,3,64]{0,3,2,1:T(8,128)} %bitcast.110), kind=kOutput, calls=%fused_computation.11 | convolution fusion | flops 860618752 | bytes 41230336 | tf_op jit(solution)/shard_map/while/body/eval_jaxpr/while/body/qhe,khe->hqk/dot_general | solution.py:158
  158.6 4.6 copy-done.7
  163.2 3.4 fusion.48
  166.6 10.1 %fusion.44 = f32[8,896,64]{1,2,0:T(8,128)} fusion(bf16[8,896,896]{2,1,0:T(8,128)(2,1)} %copy-done.7, bf16[896,8,64]{0,2,1:T(8,128)(2,1)} %get-tuple-element.869), kind=kOutput, calls=%fused_computation.113 | convolution fusion | flops 822083584 | bytes 15597568 | tf_op jit(solution)/shard_map/while/body/eval_jaxpr/while/body/hqk,khe->qhe/dot_general | solution.py:164
  176.7 3.7 copy.59
  180.4 3.8 copy.58
  184.2 3.7 copy.57
  187.9 2.1 broadcast.423
  190.0 2.1 broadcast.423.clone.1
  192.0 2.1 broadcast.423.clone.2
  194.2 13.5 %while.70 = (s32[]{:T(128)}, f32[896,8,64]{2,1,0:T(8,128)}, f32[896,8,64]{2,1,0:T(8,128)}, f32[896,8,64]{2,1,0:T(8,128)}, s32[]{:T(128)}, /*index=5*/f32[8,896,6...) while((s32[]{:T(128)}, f32[896,8,64]{2,1,0:T(8,128)}, f32[896,8,64]{2,1,0:T(8,128)}, ...), condition=%wide.region_17.18_spmd, body=%wide.region_16.17_spmd.sunk | while | flops 2293762 | bytes 23855224 | solution.py:194
  194.2 9.1 %bitcast_add_fusion.9 = (f32[896,8,64]{2,1,0:T(8,128)}, f32[896,8,64]{2,1,0:T(8,128)}) fusion(f32[896,8,64]{2,1,0:T(8,128)} %get-tuple-element.831, f32[8,896,64]{2,0,1:T(8,128)} %get-tuple-element.844, f32[896,8,64]{2,1,0:T(8,128)} %get-tuple-element.830, f32[8,896,64]{2,0,1:T(8,128)} %get-tuple-element.843), kind=kLoop, calls=%fused_computation.2.clone.1 | loop fusion | flops 1376256 | bytes 11010048 | tf_op jit(solution)/shard_map/while/body/eval_jaxpr/while/body/add | solution.py:185
  203.3 4.2 bitcast_add_fusion.8
  207.7 3.7 copy.61
  211.5 2.5 multiply_reduce_fusion.3
  214.0 3.7 copy.60
  217.7 2.6 multiply_reduce_fusion.4
  220.9 4.0 multiply_reduce_fusion.1
  226.4 3.0 fusion.22
  229.3 3.4 copy.62
  232.7 2.1 pad_maximum_fusion
  236.6 3.1 fusion.45
  239.7 4.2 fusion.38
  243.9 22.1 %convert_reduce_fusion = (f32[2048]{0:T(1024)S(1)}, bf16[896,2048]{1,0:T(8,128)(2,1)S(1)}, f32[896,2048]{1,0:T(8,128)}) fusion(f32[896,2048]{1,0:T(8,128)S(1)} %fusion.38, f32[2048]{0:T(1024)S(1)} %copy-done.48, bf16[896,1024]{1,0:T(8,128)(2,1)S(1)} %copy-done.55, bf16[2048,1024]{1,0:T(8,128)(2,1)S(1)} %copy-done.53), kind=kOutput, calls=%fused_computation.16 | convolution fusion | flops 3895719936 | bytes 24395776 | tf_op jit(solution)/shard_map/dot_general | solution.py:27
  266.1 1.8 copy-done.57
  267.9 5.2 add_convert_fusion.1
  273.1 3.4 copy.54
  276.5 7.9 multiply_convert_fusion.1
  284.4 3.9 fusion.43
  288.4 2.5 add_convert_fusion.2
  291.0 4.5 fusion.46
  295.5 6.5 fusion.37
  302.0 6.9 fusion.47
  308.9 7.3 fusion.36
  316.3 3.8 fusion.10
  320.1 2.4 fusion.20
  322.6 5.3 all-reduce.4
  327.9 3.7 convert_reduce_fusion.2
  331.5 63.3 %all-reduce.2 = (f32[512]{0:T(512)}, f32[2,64]{1,0:T(2,128)}, f32[2048]{0:T(1024)}, f32[512]{0:T(512)}) all-reduce(f32[512]{0:T(512)S(1)} %get-tuple-element.524, f32[2,64]{1,0:T(2,128)S(1)} %get-tuple-element.587, f32[2048]{0:T(1024)S(1)} %get-tuple-element.588, ...), channel_id=1, replica_groups=mesh['batch'=16,'head'=2] {'batch'}, use_global_device_ids=true, to_apply=%region_28.29 | all-reduce | flops 3200 | bytes 25600 | tf_op jit(solution)/shard_map/psum | solution.py:298
  394.9 2.7 add_convert_fusion.5
  397.5 385.3 %all-reduce.7.cloned.1.call-done = (f32[1024,1536]{1,0:T(8,128)}, f32[512,1024]{1,0:T(8,128)}, f32[1024,2048]{1,0:T(8,128)}, f32[2048,1024]{1,0:T(8,128)}) async-done(((f32[1024,1536]{1,0:T(8,128)}, f32[512,1024]{1,0:T(8,128)}, f32[1024,2048]{1,0:T(8,128)}, f32[2048,1024]{1,0:T(8,128)}), (f32[1024,1536]{1,0:T(8,128)}, f32[512,1024]{1,0:T(8,128)}, f32[1024,2048]{1,0:T(8,128)}, ...) | async-done | bytes 25165840 | tf_op jit(solution)/shard_map/psum | solution.py:298
  782.8 6.6 copy.121
  791.7 4.3 copy.123
  797.3 3.4 copy.124
  (169 shorter events, 19.8 us)
Async XLA Ops:
  7.2 39.4 %copy-start = (bf16[1024,1536]{1,0:T(8,128)(2,1)S(1)}, bf16[1024,1536]{1,0:T(8,128)(2,1)}, u32[]{:S(2)}) copy-start(bf16[1024,1536]{1,0:T(8,128)(2,1)} %param.22) | copy-start | bytes 9437188
  7.2 39.4 %copy-start.50 = (f32[1024]{0:T(1024)S(1)}, f32[1024]{0:T(1024)}, u32[]{:S(2)}) copy-start(f32[1024]{0:T(1024)} %param.21) | copy-start | bytes 12292
  7.2 35.3 %all-gather.3.cloned.1.call-start = ((), (), s32[]{:S(2)}) async-start(), calls=%async_computation.2 | async-start | bytes 2752512 | tf_op jit(solution)/shard_map/all_gather | solution.py:223
  7.9 99.4 %all-gather.5.cloned.1.call-start = ((), (), s32[]{:S(2)}) async-start(), calls=%async_computation.4 | async-start | bytes 2752512 | tf_op jit(solution)/shard_map/all_gather | solution.py:244
  8.7 311.4 %reduce-scatter.5.cloned.1.call-start = ((), (), s32[]{:S(2)}) async-start(), calls=%async_computation.5 | async-start | bytes 2752512 | tf_op jit(solution)/shard_map/reduce_scatter | solution.py:281
  16.7 35.7 %copy-start.46 = (f32[64]{0:T(128)}, f32[64]{0:T(128)S(1)}, u32[]{:S(2)}) copy-start(f32[64]{0:T(128)S(1)} %get-tuple-element.600) | copy-start | bytes 772
  16.7 36.1 %copy-start.44 = (f32[64]{0:T(128)}, f32[64]{0:T(128)S(1)}, u32[]{:S(2)}) copy-start(f32[64]{0:T(128)S(1)} %get-tuple-element.599) | copy-start | bytes 772
  42.5 4.1 copy-start.11
  44.4 6.0 copy-start.42
  46.6 3.9 copy-start.40
  50.5 3.0 copy-start.8
  50.7 2.1 copy-start.5
  50.9 2.6 copy-start.25
  51.1 1.1 copy-start.33
  51.2 2.3 copy-start.31
  52.2 1.3 copy-start.23
  52.4 1.0 copy-start.35
  52.8 11.4 %copy-start.1 = (bf16[896,8,64]{0,2,1:T(8,128)(2,1)}, bf16[896,8,64]{0,2,1:T(8,128)(2,1)S(1)}, u32[]{:S(2)}) copy-start(bf16[896,8,64]{0,2,1:T(8,128)(2,1)S(1)} %multiply_convert_fusion.4) | copy-start | bytes 2752516
  53.8 10.4 %copy-start.3 = (bf16[896,8,64]{0,2,1:T(8,128)(2,1)}, bf16[896,8,64]{0,2,1:T(8,128)(2,1)S(1)}, u32[]{:S(2)}) copy-start(bf16[896,8,64]{0,2,1:T(8,128)(2,1)S(1)} %multiply_convert_fusion.3) | copy-start | bytes 2752516
  53.8 10.4 %copy-start.37 = (pred[896]{0:T(1024)(128)(4,1)S(1)}, pred[896]{0:T(1024)(128)(4,1)}, u32[]{:S(2)}) copy-start(pred[896]{0:T(1024)(128)(4,1)} %constant.342) | copy-start | bytes 2692
  53.8 10.4 %copy-start.38 = (pred[896]{0:T(1024)(128)(4,1)S(1)}, pred[896]{0:T(1024)(128)(4,1)}, u32[]{:S(2)}) copy-start(pred[896]{0:T(1024)(128)(4,1)} %constant.343) | copy-start | bytes 2692
  53.8 10.4 %copy-start.39 = (pred[896]{0:T(1024)(128)(4,1)S(1)}, pred[896]{0:T(1024)(128)(4,1)}, u32[]{:S(2)}) copy-start(pred[896]{0:T(1024)(128)(4,1)} %constant.344) | copy-start | bytes 2692
  107.3 4.1 copy-start.28
  143.9 19.3 %copy-start.2 = (bf16[896,8,64]{0,2,1:T(8,128)(2,1)S(1)}, bf16[896,8,64]{0,2,1:T(8,128)(2,1)}, u32[]{:S(2)}) copy-start(bf16[896,8,64]{0,2,1:T(8,128)(2,1)} %get-tuple-element.868) | copy-start | bytes 2752516
  158.6 4.6 copy-start.7
  194.2 9.1 %copy-start.4 = (f32[8,896,64]{2,0,1:T(8,128)S(1)}, f32[8,896,64]{2,0,1:T(8,128)}, u32[]{:S(2)}) copy-start(f32[8,896,64]{2,0,1:T(8,128)} %get-tuple-element.842) | copy-start | bytes 5505028 | tf_op jit(solution)/shard_map/while/body/eval_jaxpr/while
  207.7 3.8 copy-start.24
  207.7 3.8 copy-start.45
  207.7 6.2 copy-start.36
  213.9 3.8 copy-start.26
  214.0 3.8 copy-start.47
  214.0 6.4 copy-start.34
  214.0 6.4 copy-start.30
  214.0 6.4 copy-start.32
  217.7 2.7 copy-start.6
  217.7 3.2 copy-start.9
  220.9 4.0 copy-start.10
  235.0 1.5 copy-start.19
  236.6 3.1 copy-start.12
  236.6 3.1 copy-start.41
  236.6 3.1 copy-start.43
  236.6 3.1 copy-start.51
  236.6 3.1 copy-start.52
  239.7 4.2 copy-start.48
  239.7 4.2 copy-start.53
  239.7 4.2 copy-start.55
  243.9 22.1 %copy-start.15 = (f32[896,2048]{1,0:T(8,128)}, f32[896,2048]{1,0:T(8,128)S(1)}, u32[]{:S(2)}) copy-start(f32[896,2048]{1,0:T(8,128)S(1)} %fusion.38) | copy-start | bytes 22020100
  266.1 1.8 copy-start.57
  273.1 121.8 %reduce-scatter.3.cloned.1.call-start = ((), (), s32[]{:S(2)}) async-start(), calls=%async_computation.3 | async-start | bytes 2752512 | tf_op jit(solution)/shard_map/reduce_scatter | solution.py:235
  276.5 7.9 copy-start.54
  284.4 4.0 copy-start.17
  284.4 4.0 copy-start.16
  284.4 4.0 copy-start.22
  290.9 491.9 %all-reduce.7.cloned.1.call-start = ((), (), s32[]{:S(2)}) async-start(), calls=%async_computation.6 | async-start | bytes 50331648 | tf_op jit(solution)/shard_map/psum | solution.py:298
  291.0 4.6 copy-start.13
  291.0 4.6 copy-start.20
  295.5 6.5 copy-start.18
  295.5 6.5 copy-start.56
  302.0 6.9 copy-start.58
  320.1 74.8 %copy-start.49 = (f32[512]{0:T(512)S(1)}, f32[512]{0:T(512)}, u32[]{:S(2)}) copy-start(f32[512]{0:T(512)} %param.28) | copy-start | bytes 6148
  782.8 6.6 copy-start.21
  782.8 8.9 %copy-start.14 = (f32[1024,2048]{1,0:T(8,128)S(1)}, f32[1024,2048]{1,0:T(8,128)}, u32[]{:S(2)}) copy-start(f32[1024,2048]{1,0:T(8,128)} %get-tuple-element.852) | copy-start | bytes 25165828
  789.4 6.5 slice-start
  791.7 5.6 slice-start.1
  (2 other events, 1.9 us)
Sparse Core Ops, SparseCore 0:
  9.6 32.8 all-gather.2
  44.0 30.1 all-gather.4
  273.2 28.9 reduce-scatter.4
  304.4 29.2 reduce-scatter.2
  339.6 443.2 all-reduce.6
where the time goes:
time: 815 us; the launch traced here: 808 us
  waiting for transfers between devices  407 us (50%)
  matrix products  151 us (19%)
  other arithmetic  88.3 us (11%)
  local copies, waits for them, and re-layouts  73.4 us (9%)
  blocking collectives  68.6 us (8%)
  between operations  18.3 us (2%)
    psum x1, waiting for transfers between devices, on_device(): lax.psum((grad_ln_local, grad_wqkv, grad_wo, grad_wup, grad_b_up, grad_wd...  385 us
    psum x1, blocking collectives, on_device(): lax.psum((grad_ln_local, grad_wqkv, grad_wo, grad_wup, grad_b_up, grad_wd...  63.3 us
    dot_general x8, matrix products, contract(): lax.dot_general(left, right, (((left_dim,), (right_dim,)), ((), ())), pre...  58.7 us
    unnamed x124, local copies, waits for them, and re-layouts  29.1 us
    dot_general x2, matrix products, block_scores(): jnp.einsum('qhe,khe->hqk', query_block, key_norm, preferred_element_type=...  24.3 us
    while x6, local copies, waits for them, and re-layouts, one_block(): lax.fori_loop(first_block, stop_block, inner, initial)  21.9 us
    all_gather x1, waiting for transfers between devices, on_device(): gathered = lax.all_gather(tokens, 'head', axis=1, tiled=True)  20.2 us
  transfers between devices with their start and end apart: 5, of which 2 were waited for; matrix products, arithmetic and copies ran while one was open for 16% of the time, Pallas kernels for 0%

commit v1 on v0

v1 whole, which is shorter than its diff:
```python
import functools

import jax
import jax.numpy as jnp
from jax import lax
from jax.experimental import pallas as pl
from jax.experimental.pallas import tpu as pltpu
from jax.sharding import PartitionSpec as P

HD = 64
EPSILON = 1e-06
FAR = -16384.0
LOW = jnp.bfloat16
WIDE = jnp.float32
MIB = 1024 * 1024


def contract(left, right, left_dim, right_dim):
    return lax.dot_general(
        left, right, (((left_dim,), (right_dim,)), ((), ())), preferred_element_type=WIDE
    )


def swap(values, axis):
    return lax.ppermute(values, axis, [(0, 1), (1, 0)])


def both_halves(mine, other, first, dim):
    return jnp.where(
        first,
        jnp.concatenate([mine, other], axis=dim),
        jnp.concatenate([other, mine], axis=dim),
    )


def mlp_body(normed_ref, w_ref, b_ref, hidden_ref, slope_ref):
    pre = jnp.dot(normed_ref[...], w_ref[...], preferred_element_type=WIDE) + b_ref[...]
    cdf = 0.5 * (1.0 + lax.erf(pre * (0.5**0.5)))
    density = jnp.exp(-0.5 * pre * pre) * 0.3989422804014327
    hidden_ref[...] = (pre * cdf).astype(LOW)
    slope_ref[...] = (cdf + pre * density).astype(LOW)


def mlp_forward(normed, w_up, b_up):
    rows, width = normed.shape
    units = w_up.shape[1]
    block = 256
    return pl.pallas_call(
        mlp_body,
        grid=(units // block,),
        in_specs=[
            pl.BlockSpec((rows, width), lambda i: (0, 0)),
            pl.BlockSpec((width, block), lambda i: (0, i)),
            pl.BlockSpec((1, block), lambda i: (0, i)),
        ],
        out_specs=[
            pl.BlockSpec((rows, block), lambda i: (0, i)),
            pl.BlockSpec((rows, block), lambda i: (0, i)),
        ],
        out_shape=[
            jax.ShapeDtypeStruct((rows, units), LOW),
            jax.ShapeDtypeStruct((rows, units), LOW),
        ],
        compiler_params=pltpu.CompilerParams(vmem_limit_bytes=16 * MIB),
        cost_estimate=pl.CostEstimate(
            flops=2 * rows * width * units,
            bytes_accessed=2 * (rows * width + width * units + 2 * rows * units),
            transcendentals=2 * rows * units,
        ),
        name="mlp_forward",
    )(normed, w_up, b_up.reshape(1, units))


def norm_body(side_ref, mine_ref, other_ref, gain_ref, normed_ref, stats_ref):
    mine = mine_ref[...].astype(WIDE)
    other = other_ref[...].astype(WIDE)
    width = 2 * mine.shape[1]
    half = mine.shape[1]
    center = (
        jnp.sum(mine, axis=1, keepdims=True) + jnp.sum(other, axis=1, keepdims=True)
    ) / width
    mine = mine - center
    other = other - center
    spread = (
        jnp.sum(mine * mine, axis=1, keepdims=True)
        + jnp.sum(other * other, axis=1, keepdims=True)
    ) / width
    scaled = lax.rsqrt(spread + EPSILON)
    first = side_ref[0] == 0
    left = jnp.where(first, mine, other)
    right = jnp.where(first, other, mine)
    normed_ref[:, 0:half] = (left * scaled * gain_ref[:, 0:half]).astype(LOW)
    normed_ref[:, half:width] = (right * scaled * gain_ref[:, half:width]).astype(LOW)
    lane = lax.broadcasted_iota(jnp.int32, stats_ref.shape, 1)
    stats_ref[...] = jnp.where(lane == 0, center, scaled)


def input_norm(side, mine, other, gain):
    rows, half = mine.shape
    block = 224
    return pl.pallas_call(
        norm_body,
        grid_spec=pltpu.PrefetchScalarGridSpec(
            num_scalar_prefetch=1,
            grid=(rows // block,),
            in_specs=[
                pl.BlockSpec((block, half), lambda i, s: (i, 0)),
                pl.BlockSpec((block, half), lambda i, s: (i, 0)),
                pl.BlockSpec((1, 2 * half), lambda i, s: (0, 0)),
            ],
            out_specs=[
                pl.BlockSpec((block, 2 * half), lambda i, s: (i, 0)),
                pl.BlockSpec((block, 128), lambda i, s: (i, 0)),
            ],
        ),
        out_shape=[
            jax.ShapeDtypeStruct((rows, 2 * half), LOW),
            jax.ShapeDtypeStruct((rows, 128), WIDE),
        ],
        cost_estimate=pl.CostEstimate(
            flops=20 * rows * half, bytes_accessed=10 * rows * half, transcendentals=rows
        ),
        name="input_norm",
    )(side, mine, other, gain.reshape(1, 2 * half))


def slope_body(piece_ref, w_ref, slope_ref, grad_pre_ref, bias_ref):
    back = lax.dot_general(
        piece_ref[...], w_ref[...], (((1,), (1,)), ((), ())), preferred_element_type=WIDE
    )
    low = (back * slope_ref[...].astype(WIDE)).astype(LOW)
    grad_pre_ref[...] = low
    bias_ref[...] = jnp.sum(low.astype(WIDE), axis=0, keepdims=True)


def mlp_slope(piece, w_down, slope):
    rows, width = piece.shape
    units = w_down.shape[0]
    block = 256
    return pl.pallas_call(
        slope_body,
        grid=(units // block,),
        in_specs=[
            pl.BlockSpec((rows, width), lambda i: (0, 0)),
            pl.BlockSpec((block, width), lambda i: (i, 0)),
            pl.BlockSpec((rows, block), lambda i: (0, i)),
        ],
        out_specs=[
            pl.BlockSpec((rows, block), lambda i: (0, i)),
            pl.BlockSpec((1, block), lambda i: (0, i)),
        ],
        out_shape=[
            jax.ShapeDtypeStruct((rows, units), LOW),
            jax.ShapeDtypeStruct((1, units), WIDE),
        ],
        compiler_params=pltpu.CompilerParams(vmem_limit_bytes=16 * MIB),
        cost_estimate=pl.CostEstimate(
            flops=2 * rows * width * units,
            bytes_accessed=2 * (rows * width + width * units + 2 * rows * units),
            transcendentals=0,
        ),
        name="mlp_slope",
    )(piece, w_down, slope)


def first_dims(left, right):
    return lax.dot_general(left, right, (((0,), (0,)), ((), ())), preferred_element_type=WIDE)


def mlp_weights_body(down_steps, hidden_ref, piece_ref, normed_ref, grad_pre_ref, out_ref):
    step = pl.program_id(0)

    @pl.when(step < down_steps)
    def _():
        out_ref[...] = first_dims(hidden_ref[...], piece_ref[...]).astype(LOW)

    @pl.when(step >= down_steps)
    def _():
        out_ref[...] = first_dims(normed_ref[...], grad_pre_ref[...]).astype(LOW)


def mlp_weights(hidden, piece, normed, grad_pre):
    rows, units = hidden.shape
    width = piece.shape[1]
    block = 512
    down = units // block
    across = width // block
    halves = units // width

    def later(i):
        return jnp.maximum(i - down, 0)

    return pl.pallas_call(
        functools.partial(mlp_weights_body, down),
        grid=(down + halves * across,),
        in_specs=[
            pl.BlockSpec((rows, block), lambda i: (0, jnp.minimum(i, down - 1))),
            pl.BlockSpec((rows, width), lambda i: (0, 0)),
            pl.BlockSpec((rows, block), lambda i: (0, later(i) % across)),
            pl.BlockSpec((rows, width), lambda i: (0, later(i) // across)),
        ],
        out_specs=pl.BlockSpec((block, width), lambda i: (i, 0)),
        out_shape=pltpu.HBM((2 * units, width), LOW),
        compiler_params=pltpu.CompilerParams(vmem_limit_bytes=24 * MIB),
        cost_estimate=pl.CostEstimate(
            flops=4 * rows * width * units,
            bytes_accessed=2 * (2 * rows * width + 2 * rows * units + 2 * width * units),
            transcendentals=0,
        ),
        name="mlp_weights",
    )(hidden, piece, normed, grad_pre)


def heads_weights_body(normed_ref, grad_joined_ref, piece_ref, attended_ref, out_ref):
    columns = grad_joined_ref.shape[1]
    out_ref[:, 0:columns] = first_dims(normed_ref[...], grad_joined_ref[...]).astype(LOW)
    out_ref[:, columns:] = lax.dot_general(
        piece_ref[...], attended_ref[...], (((0,), (1,)), ((), ())), preferred_element_type=WIDE
    ).astype(LOW)


def heads_weights(normed, grad_joined, piece, attended_t):
    rows, width = normed.shape
    columns, inner = grad_joined.shape[1], attended_t.shape[0]
    block = 256
    return pl.pallas_call(
        heads_weights_body,
        grid=(width // block,),
        in_specs=[
            pl.BlockSpec((rows, block), lambda i: (0, i)),
            pl.BlockSpec((rows, columns), lambda i: (0, 0)),
            pl.BlockSpec((rows, block), lambda i: (0, i)),
            pl.BlockSpec((inner, rows), lambda i: (0, 0)),
        ],
        out_specs=pl.BlockSpec((block, columns + inner), lambda i: (i, 0)),
        out_shape=jax.ShapeDtypeStruct((width, columns + inner), LOW),
        compiler_params=pltpu.CompilerParams(vmem_limit_bytes=16 * MIB),
        cost_estimate=pl.CostEstimate(
            flops=2 * rows * width * (columns + inner),
            bytes_accessed=2 * (2 * rows * width + (rows + width) * (columns + inner)),
            transcendentals=0,
        ),
        name="heads_weights",
    )(normed, grad_joined, piece, attended_t)


def spread_body(columns, mlp_ref, *refs):
    heads_refs, (down_ref, up_ref, qkv_ref, out_ref) = refs[:-4], refs[-4:]
    step = pl.program_id(0)
    steps = pl.num_programs(0)

    @pl.when(step < steps // 2)
    def _():
        down_ref[...] = mlp_ref[...].astype(WIDE).reshape(down_ref.shape)

    @pl.when(step >= steps // 2)
    def _():
        up_ref[...] = mlp_ref[...].astype(WIDE).reshape(up_ref.shape)

    for number, ref in enumerate(heads_refs):
        value = ref[...].astype(WIDE).reshape(qkv_ref.shape[0], -1)
        inner = value.shape[1] - columns
        qkv_ref[:, columns * number : columns * (number + 1)] = value[:, 0:columns]
        out_ref[inner * number : inner * (number + 1), :] = jnp.transpose(value[:, columns:])


def spread(whole, n, units, columns, count):
    width = whole.shape[1]
    mlp_rows, heads_rows = 2 * units // n, width // n
    assert whole.shape[0] == n * (mlp_rows + count * heads_rows)
    steps = width // 128
    block = 2 * units // steps
    inner = width - columns
    across = 2 * width // block // 2

    def later(i):
        return jnp.maximum(i - steps // 2, 0)

    def heads_spec(number):
        skip = mlp_rows // heads_rows + number
        return pl.BlockSpec((n // steps, 1, heads_rows, width), lambda i: (i, skip, 0, 0))

    by_rows = whole.reshape(n, -1, width)
    by_parts = whole.reshape(n, -1, heads_rows, width)
    return pl.pallas_call(
        functools.partial(spread_body, columns),
        grid=(steps,),
        in_specs=[pl.BlockSpec((n // steps, mlp_rows, width), lambda i: (i, 0, 0))]
        + [heads_spec(number) for number in range(count)],
        out_specs=[
            pl.BlockSpec((block, width), lambda i: (jnp.minimum(i, steps // 2 - 1), 0)),
            pl.BlockSpec((block, width), lambda i: (later(i) % across, later(i) // across)),
            pl.BlockSpec((128, columns * count), lambda i: (i, 0)),
            pl.BlockSpec((inner * count, 128), lambda i: (0, i)),
        ],
        out_shape=[
            jax.ShapeDtypeStruct((units, width), WIDE),
            jax.ShapeDtypeStruct((width, units), WIDE),
            jax.ShapeDtypeStruct((width, columns * count), WIDE),
            jax.ShapeDtypeStruct((inner * count, width), WIDE),
        ],
        compiler_params=pltpu.CompilerParams(vmem_limit_bytes=32 * MIB),
        cost_estimate=pl.CostEstimate(
            flops=whole.size, bytes_accessed=6 * whole.size, transcendentals=0
        ),
        name="spread",
    )(by_rows, *[by_parts] * count)


def output_body(mine, side_ref, attended_ref, w_out_ref, hidden_ref, w_down_ref, *refs):
    total = jnp.dot(hidden_ref[...], w_down_ref[...], preferred_element_type=WIDE) + first_dims(
        attended_ref[...], w_out_ref[...]
    )
    if mine:
        tokens_ref, arrived_ref, bias_ref, out_ref = refs
        total = (
            tokens_ref[...].astype(WIDE) + (total + arrived_ref[...].astype(WIDE)) + bias_ref[...]
        )
    else:
        (out_ref,) = refs
    out_ref[...] = total.astype(LOW)


def output_half(mine, side, attended_t, w_out, hidden, w_down, *more):
    inner, rows = attended_t.shape
    units, width = w_down.shape
    half = width // 2
    block = rows
    flip = 0 if mine else 1

    def column(i, s):
        return (0, s[0] ^ flip)

    extra = []
    if mine:
        extra = [
            pl.BlockSpec((block, half), lambda i, s: (i, 0)),
            pl.BlockSpec((block, half), lambda i, s: (i, 0)),
            pl.BlockSpec((1, half), lambda i, s: (0, 0)),
        ]
    return pl.pallas_call(
        functools.partial(output_body, mine),
        grid_spec=pltpu.PrefetchScalarGridSpec(
            num_scalar_prefetch=1,
            grid=(rows // block,),
            in_specs=[
                pl.BlockSpec((inner, block), lambda i, s: (0, i)),
                pl.BlockSpec((inner, half), column),
                pl.BlockSpec((block, units), lambda i, s: (i, 0)),
                pl.BlockSpec((units, half), column),
                *extra,
            ],
            out_specs=pl.BlockSpec((block, half), lambda i, s: (i, 0)),
        ),
        out_shape=jax.ShapeDtypeStruct((rows, half), LOW),
        compiler_params=pltpu.CompilerParams(vmem_limit_bytes=20 * MIB),
        cost_estimate=pl.CostEstimate(
            flops=2 * rows * half * (inner + units),
            bytes_accessed=2 * (rows + half) * (inner + units) + 6 * rows * half,
            transcendentals=0,
        ),
        name="output_mine" if mine else "output_away",
    )(side, attended_t, w_out, hidden, w_down, *more)


def second_dims(left, right):
    return lax.dot_general(left, right, (((1,), (1,)), ((), ())), preferred_element_type=WIDE)


def grad_in_body(mine, side_ref, grad_joined_ref, w_qkv_ref, grad_pre_ref, w_up_ref, *refs):
    total = second_dims(grad_joined_ref[...], w_qkv_ref[...]) + second_dims(
        grad_pre_ref[...], w_up_ref[...]
    )
    if not mine:
        (away_ref,) = refs
        away_ref[...] = total.astype(LOW)
        return
    tokens_ref, arrived_ref, stats_ref, gain_ref, hat_ref, sums_ref, gain_grad_ref = refs
    total = total + arrived_ref[...].astype(WIDE)
    x_hat = (tokens_ref[...].astype(WIDE) - stats_ref[:, 0:1]) * stats_ref[:, 1:2]
    grad_hat = total * gain_ref[...]
    hat_ref[...] = grad_hat
    lane = lax.broadcasted_iota(jnp.int32, sums_ref.shape, 1)
    sums_ref[...] = jnp.where(
        lane == 0,
        jnp.sum(grad_hat, axis=1, keepdims=True),
        jnp.sum(grad_hat * x_hat, axis=1, keepdims=True),
    )
    gain_grad_ref[...] = jnp.sum(total * x_hat, axis=0, keepdims=True)


def grad_in_half(mine, side, grad_joined, w_qkv, grad_pre, w_up, *more):
    rows, columns = grad_joined.shape
    width, units = w_up.shape
    half = width // 2
    flip = 0 if mine else 1

    def picked(i, s):
        return (s[0] ^ flip, 0)

    def whole(i, s):
        return (0, 0)

    extra, outs = [], [((rows, half), LOW)]
    if mine:
        extra = [
            pl.BlockSpec((rows, half), whole),
            pl.BlockSpec((rows, half), whole),
            pl.BlockSpec((rows, 128), whole),
            pl.BlockSpec((1, half), lambda i, s: (0, s[0])),
        ]
        outs = [((rows, half), WIDE), ((rows, 128), WIDE), ((1, half), WIDE)]
    return pl.pallas_call(
        functools.partial(grad_in_body, mine),
        grid_spec=pltpu.PrefetchScalarGridSpec(
            num_scalar_prefetch=1,
            grid=(1,),
            in_specs=[
                pl.BlockSpec((rows, columns), whole),
                pl.BlockSpec((half, columns), picked),
                pl.BlockSpec((rows, units), whole),
                pl.BlockSpec((half, units), picked),
                *extra,
            ],
            out_specs=[pl.BlockSpec(shape, whole) for shape, _ in outs],
        ),
        out_shape=[jax.ShapeDtypeStruct(shape, kind) for shape, kind in outs],
        compiler_params=pltpu.CompilerParams(vmem_limit_bytes=28 * MIB),
        cost_estimate=pl.CostEstimate(
            flops=2 * rows * half * (columns + units),
            bytes_accessed=2 * (rows + half) * (columns + units) + 10 * rows * half,
            transcendentals=0,
        ),
        name="grad_in_mine" if mine else "grad_in_away",
    )(side, grad_joined, w_qkv, grad_pre, w_up, *more)


def finish_body(cotangent_ref, tokens_ref, stats_ref, hat_ref, sums_ref, other_ref, out_ref):
    width = 2 * tokens_ref.shape[1]
    scaled = stats_ref[:, 1:2]
    x_hat = (tokens_ref[...].astype(WIDE) - stats_ref[:, 0:1]) * scaled
    sums = (sums_ref[:, 0:2] + other_ref[...]) / width
    out_ref[...] = (
        cotangent_ref[...].astype(WIDE)
        + scaled * (hat_ref[...] - sums[:, 0:1] - x_hat * sums[:, 1:2])
    ).astype(LOW)


def grad_in_finish(cotangent, tokens, stats, hat, sums, other):
    rows, half = tokens.shape
    block = 224

    def rows_of(columns):
        return pl.BlockSpec((block, columns), lambda i: (i, 0))

    return pl.pallas_call(
        finish_body,
        grid=(rows // block,),
        in_specs=[rows_of(c) for c in (half, half, 128, half, 128, 2)],
        out_specs=rows_of(half),
        out_shape=jax.ShapeDtypeStruct((rows, half), LOW),
        cost_estimate=pl.CostEstimate(
            flops=10 * rows * half, bytes_accessed=10 * rows * half, transcendentals=0
        ),
        name="grad_in_finish",
    )(cotangent, tokens, stats, hat, sums, other)


def part_norm(values):
    center = jnp.mean(values, axis=0, keepdims=True)
    shifted = values - center
    scaled = lax.rsqrt(jnp.mean(shifted * shifted, axis=0, keepdims=True) + EPSILON)
    return shifted * scaled, scaled


def part_norm_back(grad, normal, scaled, gain):
    g = grad * gain
    inner = jnp.mean(g * normal, axis=0, keepdims=True)
    return scaled * (g - jnp.mean(g, axis=0, keepdims=True) - normal * inner)


def lane_fold(values):
    total = values[:, 0:128]
    for start in range(128, values.shape[1], 128):
        total = total + values[:, start : start + 128]
    return total


def attention_body(rows, tiles, joined_ref, grad_ref, gain_ref, query_mark_ref, key_mark_ref,
                   attended_ref, grad_joined_ref, gain_grad_ref, key_grad, value_grad):
    factor = float(HD) ** (-0.5)
    gain_query = gain_ref[0:HD, :]
    gain_key = gain_ref[HD : 2 * HD, :]
    pieces = []
    gain_sum_query = jnp.zeros((HD, 128), WIDE)
    gain_sum_key = jnp.zeros((HD, 128), WIDE)
    one_mark = jnp.where(lax.broadcasted_iota(jnp.int32, (HD, rows), 0) < 2, 1.0, 0.0).astype(LOW)
    for head in range(2):
        base = head * 3 * HD
        query_hat, query_scale = part_norm(joined_ref[base : base + HD, :])
        key_hat, key_scale = part_norm(joined_ref[base + HD : base + 2 * HD, :])
        value_t = joined_ref[base + 2 * HD : base + 3 * HD, :].astype(LOW)
        query_t = (query_hat * gain_query).astype(LOW)
        key_t = (key_hat * gain_key).astype(LOW)
        grad_t = grad_ref[head * HD : (head + 1) * HD, :]
        query_aug = jnp.concatenate([query_t * factor, query_mark_ref[...]], axis=0)
        key_aug = jnp.transpose(jnp.concatenate([key_t, key_mark_ref[...]], axis=0))
        value_aug_t = jnp.concatenate([value_t, one_mark], axis=0)
        value_aug = jnp.transpose(value_aug_t)
        query_grads = []
        for number, (q0, q1, k0, k1) in enumerate(tiles):
            scores = jnp.dot(key_aug[k0:k1], query_aug[:, q0:q1], preferred_element_type=WIDE)
            terms = jnp.exp(scores)
            terms_low = terms.astype(LOW)
            summed = jnp.dot(value_aug_t[:, k0:k1], terms_low, preferred_element_type=WIDE)
            inverse = 1.0 / summed[HD : HD + 1, :]
            attended = summed[0:HD, :] * inverse
            attended_ref[head * HD : (head + 1) * HD, q0:q1] = attended.astype(LOW)
            grad_tile = grad_t[:, q0:q1].astype(WIDE)
            row_inner = jnp.sum(grad_tile * attended, axis=0, keepdims=True)
            inner_high = row_inner.astype(LOW)
            inner_low = (row_inner - inner_high.astype(WIDE)).astype(LOW)
            place = lax.broadcasted_iota(jnp.int32, (HD, q1 - q0), 0)
            inner_mark = jnp.where(
                place == 0,
                -inner_high.astype(WIDE),
                jnp.where(place == 1, -inner_low.astype(WIDE), 0.0),
            ).astype(LOW)
            grad_aug = jnp.concatenate([grad_t[:, q0:q1], inner_mark], axis=0)
            shifted = jnp.dot(value_aug[k0:k1], grad_aug, preferred_element_type=WIDE)
            grad_scores = (terms * shifted).astype(LOW)
            query_grads.append(
                jnp.dot(key_t[:, k0:k1], grad_scores, preferred_element_type=WIDE)
                * (inverse * factor)
            )
            query_rows = jnp.transpose(
                jnp.concatenate(
                    [query_t[:, q0:q1].astype(WIDE) * (inverse * factor), grad_tile * inverse],
                    axis=0,
                ).astype(LOW)
            )
            key_term = jnp.dot(grad_scores, query_rows, preferred_element_type=WIDE)
            value_term = jnp.dot(terms_low, query_rows, preferred_element_type=WIDE)
            if number == 0:
                key_grad[k0:k1, :] = key_term
                value_grad[k0:k1, :] = value_term
                key_grad[k1:rows, :] = jnp.zeros((rows - k1, 2 * HD), WIDE)
                value_grad[k1:rows, :] = jnp.zeros((rows - k1, 2 * HD), WIDE)
            else:
                key_grad[k0:k1, :] += key_term
                value_grad[k0:k1, :] += value_term
        lane = lax.broadcasted_iota(jnp.int32, (rows, 2 * HD), 1)
        joint = jnp.transpose(jnp.where(lane < HD, key_grad[...], value_grad[...]))
        query_grad = jnp.concatenate(query_grads, axis=1)
        key_grad_t = joint[0:HD, :]
        gain_sum_query += lane_fold(query_grad * query_hat)
        gain_sum_key += lane_fold(key_grad_t * key_hat)
        pieces += [
            part_norm_back(query_grad, query_hat, query_scale, gain_query),
            part_norm_back(key_grad_t, key_hat, key_scale, gain_key),
            joint[HD : 2 * HD, :],
        ]
    grad_joined_ref[...] = jnp.transpose(jnp.concatenate(pieces, axis=0)).astype(LOW)

    @pl.when(pl.program_id(0) == 0)
    def _():
        gain_grad_ref[...] = jnp.zeros_like(gain_grad_ref)

    gain_grad_ref[...] += jnp.concatenate([gain_sum_query, gain_sum_key], axis=0)


def attention(joined_t, grad_t, gains, query_mark, key_mark, start, heads):
    rows = joined_t.shape[1]
    width = heads * 3 * HD
    skip = start // 2
    slot = rows // 4
    far = 3 * slot
    tiles = ((0, 512, 0, far), (512, 768, 0, rows), (768, rows, far, rows))
    return pl.pallas_call(
        functools.partial(attention_body, rows, tiles),
        grid=(heads // 2,),
        in_specs=[
            pl.BlockSpec((6 * HD, rows), lambda i: (i + skip, 0)),
            pl.BlockSpec((2 * HD, rows), lambda i: (i + skip, 0)),
            pl.BlockSpec((2 * HD, 1), lambda i: (0, 0)),
            pl.BlockSpec((HD, rows), lambda i: (0, 0)),
            pl.BlockSpec((HD, rows), lambda i: (0, 0)),
        ],
        out_specs=[
            pl.BlockSpec((2 * HD, rows), lambda i: (i, 0)),
            pl.BlockSpec((rows, 6 * HD), lambda i: (0, i)),
            pl.BlockSpec((2 * HD, 128), lambda i: (0, 0)),
        ],
        out_shape=[
            jax.ShapeDtypeStruct((heads * HD, rows), LOW),
            jax.ShapeDtypeStruct((rows, width), LOW),
            jax.ShapeDtypeStruct((2 * HD, 128), WIDE),
        ],
        scratch_shapes=[
            pltpu.VMEM((rows, 2 * HD), WIDE),
            pltpu.VMEM((rows, 2 * HD), WIDE),
        ],
        compiler_params=pltpu.CompilerParams(vmem_limit_bytes=28 * MIB),
        cost_estimate=pl.CostEstimate(
            flops=heads * 20 * rows * rows * HD,
            bytes_accessed=rows * width * 6 + heads * HD * rows * 4,
            transcendentals=heads * rows * rows,
        ),
        name="attention_both",
    )(joined_t, grad_t, gains, query_mark, key_mark)


def ring_order(n):
    if n % 4:
        return list(range(n))
    up = [z * 4 + c for z in range(n // 4) for c in range(2)]
    down = [z * 4 + 2 + c for z in reversed(range(n // 4)) for c in range(2)]
    return up + down


def ring_scatter(values, n):
    return lax.psum_scatter(
        values, "batch", scatter_dimension=0, tiled=True, axis_index_groups=[ring_order(n)]
    )


def ring_gather(own, n):
    return lax.all_gather(own, "batch", axis=0, tiled=True, axis_index_groups=[ring_order(n)])


def send(values, pairs):
    return lax.ppermute(values, "batch", pairs)


def exchange(values, bit, n):
    return send(values, [(i, i ^ bit) for i in range(n)])


def added(left, right):
    return (left.astype(WIDE) + right.astype(WIDE)).astype(LOW)


def then(done, *values):
    return lax.optimization_barrier((done, values))[1]


def ring_view(values, n):
    bits = max(n.bit_length() - 3, 0)
    return values.reshape((2,) + (2,) * bits + (2, values.shape[0] // n, values.shape[1]))


def ring_half(bit, place, n):
    dims = n.bit_length()
    mine = (place // bit) % 2
    if bit == 1:
        return dims - 2, mine
    if bit == 2:
        return 0, mine
    return dims - 1 - bit.bit_length() + 1, mine ^ ((place // 2) % 2)


def pair_send(values, bit, place, n):
    dim, mine = ring_half(bit, place, n)
    return exchange(lax.dynamic_slice_in_dim(values, 1 - mine, 1, dim), bit, n)


def pair_add(values, arrived, bit, place, n):
    dim, mine = ring_half(bit, place, n)
    return added(lax.dynamic_slice_in_dim(values, mine, 1, dim), arrived)


def small_step(values, bit, n):
    return values + exchange(values, bit, n)


def on_device(n_batch, tokens, ln_gain, w_qkv, qk_gain, w_out, w_up, b_up, w_down, b_out,
              cotangent, slot_image, token_valid):
    rows, half = tokens.shape
    width = 2 * half
    slots = slot_image.shape[0]
    slot_rows = rows // slots
    side = lax.axis_index("head")
    first = side == 0

    other_tokens = swap(tokens, "head")
    held, _ = lax.optimization_barrier((cotangent, other_tokens))
    other_cotangent = swap(held, "head")

    place = lax.axis_index("batch")
    sides = jnp.reshape(side, (1,)).astype(jnp.int32)
    normed, stats = input_norm(sides, tokens, other_tokens, ln_gain)
    hidden, slope = mlp_forward(normed, w_up, b_up)
    piece = both_halves(cotangent, other_cotangent, first, 1)
    grad_pre, grad_b_up = mlp_slope(piece, w_down, slope)
    mlp_part = mlp_weights(hidden, piece, normed, grad_pre)
    mlp_own = ring_scatter(mlp_part, n_batch)

    token_image = jnp.repeat(slot_image, slot_rows, total_repeat_length=rows)
    ids = lax.broadcasted_iota(jnp.int32, (HD, rows), 0)
    same = token_image[None, :] == ids
    query_mark = jnp.where(same, 1.0, 0.0).astype(LOW)
    key_mark = jnp.where(same & (token_valid == 1)[None, :], 0.0, FAR)
    key_mark = jnp.where(ids < slots, key_mark, 0.0).astype(LOW)
    gains = qk_gain.reshape(-1, 1)
    columns, inner = w_qkv.shape[1] // 2, w_out.shape[0] // 2
    heads = columns // (3 * HD)
    bits = []
    while 4 * 2 ** len(bits) < n_batch:
        bits.append(4 * 2 ** len(bits))

    def heads_part(number, normed, piece):
        joined_t = contract(w_qkv[:, number * columns : (number + 1) * columns], normed, 0, 1)
        grad_t = contract(w_out[number * inner : (number + 1) * inner], piece, 1, 1).astype(LOW)
        return joined_t, grad_t

    def heads_both(joined_t, grad_t, normed, piece):
        attended_t, grad_joined, gain_grad = attention(
            joined_t, grad_t, gains, query_mark, key_mark, 0, heads
        )
        weights = heads_weights(normed, grad_joined, piece, attended_t)
        return attended_t, grad_joined, gain_grad, weights

    ready = heads_part(0, *then(mlp_part, normed, piece))
    att0, join0, gain0, part0 = heads_both(*ready, normed, piece)
    part0 = ring_view(part0, n_batch)
    core0 = pair_send(part0, 1, place, n_batch)
    ready = heads_part(1, *then(part0, normed, piece))
    (core0,) = then(ready, core0)
    part0 = pair_add(part0, core0, 1, place, n_batch)
    over0 = pair_send(part0, 2, place, n_batch)
    att1, join1, gain1, part1 = heads_both(*then(part0, *ready), normed, piece)
    part1 = ring_view(part1, n_batch)
    core1 = pair_send(part1, 1, place, n_batch)
    (over0,) = then(part1, over0)
    part0 = pair_add(part0, over0, 2, place, n_batch)
    sent0 = pair_send(part0, bits[0], place, n_batch)
    attended_t = jnp.concatenate([att0, att1], axis=0)
    grad_joined = jnp.concatenate([join0, join1], axis=1)
    back = (sides, grad_joined, w_qkv, grad_pre, w_up)
    (away_in,) = grad_in_half(False, *then(part0, *back))
    arrived_in = swap(away_in, "head")
    (core1,) = then(away_in, core1)
    part1 = pair_add(part1, core1, 1, place, n_batch)
    over1 = pair_send(part1, 2, place, n_batch)
    branch = (sides, attended_t, w_out, hidden, w_down)
    away_out = output_half(False, *then(part1, *branch))
    arrived_out = swap(away_out, "head")
    for bit, after in zip(bits, bits[1:] + [0]):
        (sent0,) = then(away_out, sent0)
        part0 = pair_add(part0, sent0, bit, place, n_batch)
        if after:
            sent0 = pair_send(part0, after, place, n_batch)
    (over1,) = then(away_out, over1)
    part1 = pair_add(part1, over1, 2, place, n_batch)
    for bit in bits:
        part1 = pair_add(part1, pair_send(part1, bit, place, n_batch), bit, place, n_batch)
    own = jnp.concatenate([mlp_own] + [p.reshape(-1, width) for p in (part0, part1)], axis=0)
    whole = ring_gather(own, n_batch)

    hat, sums, grad_ln = grad_in_half(
        True, *then(own, *back), tokens, arrived_in, stats, ln_gain.reshape(1, width)
    )
    sums_other = swap(sums[:, 0:2].T, "head").T
    gain_grad = jnp.sum(gain0 + gain1, axis=1)
    gain_grad = gain_grad + swap(gain_grad, "head")
    grad_b_out = jnp.sum(cotangent.astype(WIDE), axis=0)
    small = jnp.concatenate([grad_ln[0], grad_b_out, grad_b_up[0], gain_grad])
    output = output_half(True, *then(hat, *branch), tokens, arrived_out, b_out.reshape(1, half))
    grad_tokens = grad_in_finish(cotangent, tokens, stats, hat, sums, sums_other)
    for bit in [1, 2] + bits:
        small = small_step(small, bit, n_batch)
    units = b_up.shape[0]
    (whole,) = then((output, grad_tokens, small), whole)
    grad_wd, grad_wup, grad_wqkv, grad_wo = spread(whole, n_batch, units, columns, 2)
    return (
        output,
        grad_tokens,
        small[0:half],
        grad_wqkv,
        small[2 * half + units :].reshape(qk_gain.shape),
        grad_wo,
        grad_wup,
        small[2 * half : 2 * half + units],
        grad_wd,
        small[half : 2 * half],
    )


def solution(mesh):
    placed = (
        P("batch", "head"),
        P(),
        P(None, "head"),
        P(),
        P("head", None),
        P(None, "head"),
        P("head"),
        P("head", None),
        P("head"),
        P("batch", "head"),
        P("batch"),
        P("batch"),
    )
    return jax.shard_map(
        functools.partial(on_device, mesh.shape["batch"]),
        mesh=mesh,
        in_specs=placed,
        out_specs=(
            P("batch", "head"),
            P("batch", "head"),
            P("head"),
            P(None, "head"),
            P(),
            P("head", None),
            P(None, "head"),
            P("head"),
            P("head", None),
            P("head"),
        ),
        check_vma=False,
    )
```

time: 815 us -> 273 us (0.33)
  waiting for transfers between devices: 407 us -> 80.5 us
  matrix products: 151 us -> 8.5 us
  Pallas kernels: 0 us -> 92 us
  other arithmetic: 88.3 us -> 13.6 us
  blocking collectives: 68.6 us -> 0 us
  local copies, waits for them, and re-layouts: 73.4 us -> 39.8 us
  starting transfers between devices: 0.2 us -> 23.4 us
    psum x1 -> x0, waiting for transfers between devices: 385 us -> none  [on_device(): lax.psum((grad_ln_local, grad_wqkv, grad_wo, grad_wup, grad_b_up, grad_wd...]
    dot_general x11 -> x0, matrix products: 92.1 us -> none  [the longest x2 24.3 us: block_scores(): jnp.einsum('qhe,khe->hqk', query_block, key_norm, preferred_element_type=...]
    pallas_call x0 -> x14, Pallas kernels: none -> 92 us  [the longest x2 25.4 us: attention(): pl.pallas_call(functools.partial(attention_body, rows, tiles), grid=(head...]
    ppermute x0 -> x18, waiting for transfers between devices: none -> 70.4 us  [the longest x6 42 us: swap(): return lax.ppermute(values, axis, [(0, 1), (1, 0)])]
    psum x2 -> x0, blocking collectives: 68.6 us -> none  [the longest x1 63.3 us: on_device(): lax.psum((grad_ln_local, grad_wqkv, grad_wo, grad_wup, grad_b_up, grad_wd...]
    dot_general x8 -> x4, matrix products: 58.7 us -> 8.5 us  [contract(): lax.dot_general(left, right, (((left_dim,), (right_dim,)), ((), ())), pre...]
    reduce_sum x14 -> x2, other arithmetic: 39 us -> 1.48 us  [the longest x1 1.36 us: on_device(): grad_b_out = jnp.sum(cotangent.astype(WIDE), axis=0)]
    while x11 -> x0, local copies, waits for them, and re-layouts: 29 us -> none  [the longest x6 21.9 us: one_block(): lax.fori_loop(first_block, stop_block, inner, initial)]
  transfers between devices with their start and end apart: 5 -> 20, of which waited for: 2 -> 13; matrix products, arithmetic and copies ran while one was open for 16% -> 10% of each run, Pallas kernels for 0% -> 23%
where the time goes in v1:
time: 273 us
  Pallas kernels  92 us (34%)
  waiting for transfers between devices  80.5 us (29%)
  local copies, waits for them, and re-layouts  39.8 us (15%)
  starting transfers between devices  23.4 us (9%)
  between operations  14.8 us (5%)
  other arithmetic  13.6 us (5%)
  matrix products  8.5 us (3%)
    ppermute x6, waiting for transfers between devices, swap(): return lax.ppermute(values, axis, [(0, 1), (1, 0)])  42 us
    unnamed x122, local copies, waits for them, and re-layouts  32.5 us
    ppermute x12, waiting for transfers between devices, send(): return lax.ppermute(values, 'batch', pairs)  28.3 us
    pallas_call x2, Pallas kernels, attention(): pl.pallas_call(functools.partial(attention_body, rows, tiles), grid=(head...  25.4 us
    ppermute x12, starting transfers between devices, send(): return lax.ppermute(values, 'batch', pairs)  14.2 us
    pallas_call x1, Pallas kernels, mlp_weights(): pl.pallas_call(functools.partial(mlp_weights_body, down), grid=(down + ha...  12.3 us
    all_gather x1, waiting for transfers between devices, ring_gather(): lax.all_gather(own, 'batch', axis=0, tiled=True, axis_index_groups=[ring_...  10.1 us
    pallas_call x1, Pallas kernels, spread(): pl.pallas_call(functools.partial(spread_body, columns), grid=(steps,), in...  9.35 us
  transfers between devices with their start and end apart: 20, of which 13 were waited for; matrix products, arithmetic and copies ran while one was open for 10% of the time, Pallas kernels for 23%

profile of v1, /device:TPU:0, one launch (start us, length us, event | category | flops | bytes accessed | tf_op | source)
XLA Modules:
  0.0 272.5 jit_solution(5113246418004352745)
XLA Ops:
  7.2 3.0 %collective-permute-start = (bf16[896,512]{1,0:T(8,128)(2,1)}, bf16[896,512]{1,0:T(8,128)(2,1)S(1)}, u32[]{:S(2)}, u32[]{:S(2)}) collective-permute-start(bf16[896,512]{1,0:T(8,128)(2,1)} %tokens_ref.1), channel_id=1, source_target_pairs={{0,1},{1,0},{2,3},{3,2},{4,5},{5,4},{6,7},{7,6},{8,9},{9,8},{10,11... | collective-permute-start | bytes 2752520 | tf_op jit(solution)/shard_map/ppermute | solution.py:25
  10.2 20.6 %collective-permute-done.other_ref = bf16[896,512]{1,0:T(8,128)(2,1)S(1)} collective-permute-done((bf16[896,512]{1,0:T(8,128)(2,1)}, bf16[896,512]{1,0:T(8,128)(2,1)S(1)}, u32[]{:S(2)}, u32[]{:S(2)}) %collective-permute-start) | collective-permute-done | bytes 917536 | tf_op jit(solution)/shard_map/ppermute | solution.py:25
  30.8 1.7 collective-permute-start.1
  32.5 4.6 %input_norm.1 = (bf16[896,1024]{1,0:T(8,128)(2,1)}, f32[896,128]{1,0:T(8,128)}) custom-call(s32[1]{0:T(128)} %bitcast.side_ref, bf16[896,512]{1,0:T(8,128)(2,1)} %tokens_ref.1, bf16[896,512]{1,0:T(8,128)(2,1)} %copy-done.52, f32[1,1024]{1,0:T(1,128)} %bitcast.42), custom_call_target="tpu_custom_call" | custom-call | flops 9175040 | bytes 4587520 | tf_op jit(solution)/shard_map/input_norm/pallas_call | solution.py:101
  37.2 2.2 copy-done.1
  39.3 1.5 copy-done.22
  41.5 8.6 %mlp_forward.1 = (bf16[896,2048]{1,0:T(8,128)(2,1)S(1)}, bf16[896,2048]{1,0:T(8,128)(2,1)S(1)}) custom-call(bf16[896,1024]{1,0:T(8,128)(2,1)S(1)} %copy-done.22, bf16[1024,2048]{1,0:T(8,128)(2,1)S(1)} %copy-done.1, f32[1,2048]{1,0:T(1,128)S(1)} %bitcast.47), custom_call_target="tpu_custom_call" | custom-call | flops 3758096384 | bytes 13369344 | tf_op jit(solution)/shard_map/mlp_forward/pallas_call | solution.py:48
  50.2 2.4 collective-permute-done.1
  53.1 6.5 %mlp_slope.1 = (bf16[896,2048]{1,0:T(8,128)(2,1)S(1)}, f32[1,2048]{1,0:T(1,128)S(1)}) custom-call(bf16[896,1024]{1,0:T(8,128)(2,1)S(1)} %maximum_select_fusion.piece_ref, bf16[2048,1024]{1,0:T(8,128)(2,1)S(1)} %copy-done.4, bf16[896,2048]{1,0:T(8,128)(2,1)S(1)} %get-tuple-element.78.slope_ref), custom_call_target="tpu_custom_call" | custom-call | flops 3758096384 | bytes 13369344 | tf_op jit(solution)/shard_map/mlp_slope/pallas_call | solution.py:140
  59.6 12.3 %mlp_weights.1 = bf16[4096,1024]{1,0:T(8,128)(2,1)} custom-call(bf16[896,2048]{1,0:T(8,128)(2,1)S(1)} %get-tuple-element.116.hidden_ref, bf16[896,1024]{1,0:T(8,128)(2,1)S(1)} %maximum_select_fusion.piece_ref, bf16[896,1024]{1,0:T(8,128)(2,1)S(1)} %copy-done.23, bf16[896,2048]{1,0:T(8,128)(2,1)S(1)} %get-tuple-element.109.grad_pre_ref), custom_call_target="tpu_custom_call" | custom-call | flops 7516192768 | bytes 19398656 | tf_op jit(solution)/shard_map/mlp_weights/pallas_call | solution.py:193
  72.0 1.8 copy-done.7
  75.9 2.9 %select_select_fusion = s32[896]{0:T(1024)S(1)} fusion(pred[896]{0:T(1024)(128)(4,1)S(1)} %copy-done.59, pred[896]{0:T(1024)(128)(4,1)S(1)} %copy-done.58, pred[896]{0:T(1024)(128)(4,1)S(1)} %copy-done.57, s32[]{:T(128)} %bitcast.8, s32[]{:T(128)} %bitcast.5, s32[]{:T(128)} %bitcast.6, s32[]{:T(128)} %bitcast.7), kind=kLoop, calls=%fused_computation.34 | loop fusion | flops 2688 | bytes 6288 | tf_op jit(solution)/shard_map/jit(_take)/gather | solution.py:698
  79.7 3.5 %convolution_bitcast_fusion.1.joined_ref = f32[768,896]{1,0:T(8,128)S(1)} fusion(bf16[896,1024]{1,0:T(8,128)(2,1)} %get-tuple-element.84.normed_ref, bf16[1024,1536]{1,0:T(8,128)(2,1)S(1)} %copy-done.14), kind=kOutput, calls=%fused_computation.5 | convolution fusion | flops 1409286144 | bytes 6160384 | tf_op jit(solution)/shard_map/dot_general | solution.py:19
  83.2 12.7 %attention_both.2 = (bf16[256,896]{1,0:T(8,128)(2,1)S(1)}, bf16[896,768]{1,0:T(8,128)(2,1)S(1)}, f32[128,128]{1,0:T(8,128)S(1)}) custom-call(f32[768,896]{1,0:T(8,128)S(1)} %convolution_bitcast_fusion.1.joined_ref, bf16[256,896]{1,0:T(8,128)(2,1)S(1)} %fusion.2.grad_ref, f32[128,1]{1,0:T(8,128)S(1)} %copy-done.43, ...), custom_call_target="tpu_custom_call" | custom-call | flops 4110417920 | bytes 5046272 | tf_op jit(solution)/shard_map/attention_both/pallas_call | solution.py:579
  95.9 3.5 %heads_weights.2 = bf16[1024,1024]{1,0:T(8,128)(2,1)S(1)} custom-call(bf16[896,1024]{1,0:T(8,128)(2,1)S(1)} %copy-done.24, bf16[896,768]{1,0:T(8,128)(2,1)S(1)} %get-tuple-element.82.grad_joined_ref, bf16[896,1024]{1,0:T(8,128)(2,1)S(1)} %maximum_select_fusion.piece_ref, bf16[256,896]{1,0:T(8,128)(2,1)S(1)} %get-tuple-element.83.attended_ref), custom_call_target="tpu_custom_call" | custom-call | flops 1879048192 | bytes 7602176 | tf_op jit(solution)/shard_map/heads_weights/pallas_call | solution.py:226
  99.4 1.3 copy-done.20
  100.8 1.1 constant_dynamic-slice_fusion.7
  102.6 1.2 copy-done.15
  103.8 3.6 %convolution_bitcast_fusion.joined_ref = f32[768,896]{1,0:T(8,128)S(1)} fusion(bf16[896,1024]{1,0:T(8,128)(2,1)} %get-tuple-element.84.normed_ref, bf16[1024,1536]{1,0:T(8,128)(2,1)S(1)} %copy-done.15), kind=kOutput, calls=%fused_computation.4 | convolution fusion | flops 1409286144 | bytes 6160384 | tf_op jit(solution)/shard_map/dot_general | solution.py:19
  107.4 1.7 add_convert_fusion.1
  109.1 0.9 constant_dynamic-slice_fusion.6
  110.3 1.4 collective-permute-start.3
  111.7 12.7 %attention_both.3 = (bf16[256,896]{1,0:T(8,128)(2,1)S(1)}, bf16[896,768]{1,0:T(8,128)(2,1)S(1)}, f32[128,128]{1,0:T(8,128)S(1)}) custom-call(f32[768,896]{1,0:T(8,128)S(1)} %convolution_bitcast_fusion.joined_ref, bf16[256,896]{1,0:T(8,128)(2,1)S(1)} %fusion.3.grad_ref, f32[128,1]{1,0:T(8,128)S(1)} %copy-done.44, bf16[64,896]{1,0:T(8,128)(2,1)S(1)} %copy-done.42, ...), custom_call_target="tpu_custom_call" | custom-call | flops 4110417920 | bytes 5046272 | tf_op jit(solution)/shard_map/attention_both/pallas_call | solution.py:579
  124.4 3.5 %heads_weights.3 = bf16[1024,1024]{1,0:T(8,128)(2,1)S(1)} custom-call(bf16[896,1024]{1,0:T(8,128)(2,1)S(1)} %copy-done.25, bf16[896,768]{1,0:T(8,128)(2,1)S(1)} %get-tuple-element.89.grad_joined_ref, bf16[896,1024]{1,0:T(8,128)(2,1)S(1)} %maximum_select_fusion.piece_ref, bf16[256,896]{1,0:T(8,128)(2,1)S(1)} %get-tuple-element.90.attended_ref), custom_call_target="tpu_custom_call" | custom-call | flops 1879048192 | bytes 7602176 | tf_op jit(solution)/shard_map/heads_weights/pallas_call | solution.py:226
  127.9 1.3 copy-done.18
  129.2 1.0 constant_dynamic-slice_fusion.5
  130.5 1.6 constant_dynamic-update-slice_fusion.1
  132.7 1.4 add_convert_fusion.3
  134.9 2.1 copy-done.8
  137.0 2.0 copy-done.16
  139.0 3.5 %grad_in_away.1 = bf16[896,512]{1,0:T(8,128)(2,1)S(1)} custom-call(s32[1]{0:T(128)} %bitcast.side_ref, bf16[896,1536]{1,0:T(8,128)(2,1)S(1)} %constant_dynamic-update-slice_fusion.grad_joined_ref, bf16[1024,1536]{1,0:T(8,128)(2,1)S(1)} %copy-done.16, bf16[896,2048]{1,0:T(8,128)(2,1)S(1)} %copy-done.8, bf16[1024,2048]{1,0:T(8,128)(2,1)S(1)} %copy-done.2), custom_call_target="tpu_custom_call" | custom-call | flops 3288334336 | bytes 14680064 | tf_op jit(solution)/shard_map/grad_in_away/pallas_call | solution.py:413
  142.5 2.0 add_convert_fusion
  145.3 1.4 collective-permute-start.5
  146.8 2.6 output_away.1
  149.4 0.9 copy-done.40
  150.3 3.3 %collective-permute-done.5 = bf16[1,2,1,1,64,1024]{5,4,3,2,1,0:T(8,128)(2,1)S(1)} collective-permute-done((bf16[1,2,1,1,64,1024]{5,4,3,2,1,0:T(8,128)(2,1)S(1)}, bf16[1,2,1,1,64,1024]{5,4,3,2,1,0:T(8,128)(2,1)S(1)}, u32[]{:S(2)}, u32[]{:S(2)}) %collective-permute-start.5) | collective-permute-done | bytes 262176 | tf_op jit(solution)/shard_map/ppermute | solution.py:632
  153.6 5.0 %collective-permute-done.7 = bf16[1,2,2,1,64,1024]{5,4,3,2,1,0:T(8,128)(2,1)S(1)} collective-permute-done((bf16[1,2,2,1,64,1024]{5,4,3,2,1,0:T(8,128)(2,1)S(1)}, bf16[1,2,2,1,64,1024]{5,4,3,2,1,0:T(8,128)(2,1)S(1)}, u32[]{:S(2)}, u32[]{:S(2)}) %collective-permute-start.7) | collective-permute-done | bytes 524320 | tf_op jit(solution)/shard_map/ppermute | solution.py:632
  159.6 1.6 collective-permute-start.8
  161.3 2.8 %collective-permute-start.6 = (bf16[1,1,1,1,64,1024]{5,4,3,2,1,0:T(8,128)(2,1)S(1)}, bf16[1,1,1,1,64,1024]{5,4,3,2,1,0:T(8,128)(2,1)S(1)}, u32[]{:S(2)}, u32[]{:S(2)}) collective-permute-start(bf16[1,1,1,1,64,1024]{5,4,3,2,1,0:T(8,128)(2,1)S(1)} %constant_dynamic-slice_fusion.3), channel_id=1, source_target_pairs={{0,16},{2,18},{4,20},{6,22},{8,24},{10,26},{12,28},{14,30},{16,0},... | collective-permute-start | bytes 393224 | tf_op jit(solution)/shard_map/ppermute | solution.py:632
  164.2 5.3 %collective-permute-done.6 = bf16[1,1,1,1,64,1024]{5,4,3,2,1,0:T(8,128)(2,1)S(1)} collective-permute-done((bf16[1,1,1,1,64,1024]{5,4,3,2,1,0:T(8,128)(2,1)S(1)}, bf16[1,1,1,1,64,1024]{5,4,3,2,1,0:T(8,128)(2,1)S(1)}, u32[]{:S(2)}, u32[]{:S(2)}) %collective-permute-start.6) | collective-permute-done | bytes 131104 | tf_op jit(solution)/shard_map/ppermute | solution.py:632
  170.3 1.1 add_convert_fusion.4
  171.4 2.6 collective-permute-start.9
  174.1 6.1 %collective-permute-done.9 = bf16[1,1,1,1,64,1024]{5,4,3,2,1,0:T(8,128)(2,1)S(1)} collective-permute-done((bf16[1,1,1,1,64,1024]{5,4,3,2,1,0:T(8,128)(2,1)S(1)}, bf16[1,1,1,1,64,1024]{5,4,3,2,1,0:T(8,128)(2,1)S(1)}, u32[]{:S(2)}, u32[]{:S(2)}) %collective-permute-start.9) | collective-permute-done | bytes 131104 | tf_op jit(solution)/shard_map/ppermute | solution.py:632
  180.2 2.0 pad_maximum_fusion
  182.2 1.5 collective-permute-start.10
  184.5 1.4 convert_reduce_fusion
  185.9 16.9 %collective-permute-done.13 = f32[128]{0:T(128)S(1)} collective-permute-done((f32[128]{0:T(128)S(1)}, f32[128]{0:T(128)S(1)}, u32[]{:S(2)}, u32[]{:S(2)}) %collective-permute-start.13) | collective-permute-done | bytes 544 | tf_op jit(solution)/shard_map/ppermute | solution.py:25
  202.8 1.5 collective-permute-start.11
  204.3 2.2 copy-done.3
  206.5 2.1 copy-done.9
  208.5 1.2 copy-done.13
  209.7 2.0 copy-done.17
  211.7 1.0 copy-done.35
  212.8 3.8 %grad_in_mine.1 = (f32[896,512]{1,0:T(8,128)S(1)}, f32[896,128]{1,0:T(8,128)S(1)}, f32[1,512]{1,0:T(1,128)S(1)}) custom-call(s32[1]{0:T(128)} %bitcast.side_ref, bf16[896,1536]{1,0:T(8,128)(2,1)S(1)} %constant_dynamic-update-slice_fusion.grad_joined_ref, bf16[1024,1536]{1,0:T(8,128)(2,1)S(1)} %copy-done.17, bf16[896,2048]{1,0:T(8,128)(2,1)S(1)} %copy-done.9, ...), custom_call_target="tpu_custom_call" | custom-call | flops 3288334336 | bytes 14680064 | tf_op jit(solution)/shard_map/grad_in_mine/pallas_call | solution.py:413
  216.8 1.2 collective-permute-done.14
  218.0 4.0 %collective-permute-done.15 = f32[3200]{0:T(1024)S(1)} collective-permute-done((f32[3200]{0:T(1024)S(1)}, f32[3200]{0:T(1024)S(1)}, u32[]{:S(2)}, u32[]{:S(2)}) %collective-permute-start.15) | collective-permute-done | bytes 12832 | tf_op jit(solution)/shard_map/ppermute | solution.py:632
  223.5 2.6 collective-permute-done.16
  226.1 2.5 collective-permute-start.17
  228.7 3.6 %output_mine.1 = bf16[896,512]{1,0:T(8,128)(2,1)} custom-call(s32[1]{0:T(128)} %bitcast.side_ref, bf16[512,896]{1,0:T(8,128)(2,1)S(1)} %copy-done.27, bf16[512,1024]{1,0:T(8,128)(2,1)S(1)} %copy-done.33, bf16[896,2048]{1,0:T(8,128)(2,1)S(1)} %copy-done.12, bf16[2048,1024]{1,0:T(8,128)(2,1)S(1)} %copy-done.6, bf16[896,512]{1,0:T(8,128)(2,1)S(1)} %copy-done.13, ...), custom_call_target="tpu_custom_call" | custom-call | flops 2348810240 | bytes 9961472 | tf_op jit(solution)/shard_map/output_mine/pallas_call | solution.py:341
  232.3 2.2 collective-permute-done.12
  235.2 4.6 %grad_in_finish.1 = bf16[896,512]{1,0:T(8,128)(2,1)} custom-call(bf16[896,512]{1,0:T(8,128)(2,1)} %cotangent_ref.1, bf16[896,512]{1,0:T(8,128)(2,1)} %tokens_ref.1, f32[896,128]{1,0:T(8,128)} %get-tuple-element.111.refs_2_.stats_ref, f32[896,512]{1,0:T(8,128)} %copy-done.36, f32[896,128]{1,0:T(8,128)} %copy-done.34, f32[896,2]{1,0:T(8,128)} %bitcast.48), custom_call_target="tpu_custom_call" | custom-call | flops 4587520 | bytes 4587520 | tf_op jit(solution)/shard_map/grad_in_finish/pallas_call | solution.py:456
  241.7 10.1 %all-gather.2.cloned.1.call-done = bf16[6144,1024]{1,0:T(8,128)(2,1)} async-done(((bf16[384,1024]{1,0:T(8,128)(2,1)}), bf16[6144,1024]{1,0:T(8,128)(2,1)}) %all-gather.2.cloned.1.call-update) | async-done | bytes 12582928 | tf_op jit(solution)/shard_map/all_gather | solution.py:628
  251.8 4.6 %copy-done = bf16[6144,1024]{1,0:T(8,128)(2,1)S(1)} copy-done((bf16[6144,1024]{1,0:T(8,128)(2,1)S(1)}, bf16[6144,1024]{1,0:T(8,128)(2,1)}, u32[]{:S(2)}) %copy-start) | copy-done | bytes 12582936
  256.3 9.4 %spread.1 = (f32[2048,1024]{1,0:T(8,128)}, f32[1024,2048]{1,0:T(8,128)}, f32[1024,1536]{1,0:T(8,128)}, f32[512,1024]{1,0:T(8,128)}) custom-call(bf16[16,384,1024]{2,1,0:T(8,128)(2,1)S(1)} %bitcast.33, bf16[16,6,64,1024]{3,2,1,0:T(8,128)(2,1)S(1)} %bitcast.34, bf16[16,6,64,1024]{3,2,1,0:T(8,128)(2,1)S(1)} %bitcast.35), custom_call_target="tpu_custom_call" | custom-call | flops 6291456 | bytes 37748736 | tf_op jit(solution)/shard_map/spread/pallas_call | solution.py:285
  (157 shorter events, 14.5 us)
Async XLA Ops:
  7.2 173.1 %reduce-scatter.2.cloned.1.call-start = ((), (), s32[]{:S(2)}) async-start(), calls=%async_computation.1 | async-start | bytes 8912896 | tf_op jit(solution)/shard_map/reduce_scatter | solution.py:622
  7.2 23.6 %collective-permute-start = (bf16[896,512]{1,0:T(8,128)(2,1)}, bf16[896,512]{1,0:T(8,128)(2,1)S(1)}, u32[]{:S(2)}, u32[]{:S(2)}) collective-permute-start(bf16[896,512]{1,0:T(8,128)(2,1)} %tokens_ref.1), channel_id=1, source_target_pairs={{0,1},{1,0},{2,3},{3,2},{4,5},{5,4},{6,7},{7,6},{8,9},{9,8},{10,11... | collective-permute-start | bytes 2752520 | tf_op jit(solution)/shard_map/ppermute | solution.py:25
  30.8 21.7 %collective-permute-start.1 = (bf16[896,512]{1,0:T(8,128)(2,1)}, bf16[896,512]{1,0:T(8,128)(2,1)S(1)}, u32[]{:S(2)}, u32[]{:S(2)}) collective-permute-start(bf16[896,512]{1,0:T(8,128)(2,1)} %cotangent_ref.1), channel_id=1, source_target_pairs={{0,1},{1,0},{2,3},{3,2},{4,5},{5,4},{6,7},{7,6},{8,9},{9,8},{10,11... | collective-permute-start | bytes 2752520 | tf_op jit(solution)/shard_map/ppermute | solution.py:25
  37.2 2.2 copy-start.1
  41.5 11.0 %copy-start.48 = (bf16[896,512]{1,0:T(8,128)(2,1)S(1)}, bf16[896,512]{1,0:T(8,128)(2,1)}, u32[]{:S(2)}) copy-start(bf16[896,512]{1,0:T(8,128)(2,1)} %cotangent_ref.1) | copy-start | bytes 2752516
  41.5 11.6 %copy-start.4 = (bf16[2048,1024]{1,0:T(8,128)(2,1)S(1)}, bf16[2048,1024]{1,0:T(8,128)(2,1)}, u32[]{:S(2)}) copy-start(bf16[2048,1024]{1,0:T(8,128)(2,1)} %w_down_ref.1) | copy-start | bytes 12582916
  50.2 9.5 %copy-start.10 = (bf16[896,2048]{1,0:T(8,128)(2,1)}, bf16[896,2048]{1,0:T(8,128)(2,1)S(1)}, u32[]{:S(2)}) copy-start(bf16[896,2048]{1,0:T(8,128)(2,1)S(1)} %get-tuple-element.116.hidden_ref) | copy-start | bytes 11010052
  53.1 6.5 %copy-start.23 = (bf16[896,1024]{1,0:T(8,128)(2,1)S(1)}, bf16[896,1024]{1,0:T(8,128)(2,1)}, u32[]{:S(2)}) copy-start(bf16[896,1024]{1,0:T(8,128)(2,1)} %get-tuple-element.84.normed_ref) | copy-start | bytes 5505028
  73.8 2.0 copy-start.55
  73.8 2.1 copy-start.57
  73.8 2.1 copy-start.58
  73.8 2.1 copy-start.59
  73.8 5.0 %copy-start.31 = (bf16[512,1024]{1,0:T(8,128)(2,1)S(1)}, bf16[512,1024]{1,0:T(8,128)(2,1)}, u32[]{:S(2)}) copy-start(bf16[512,1024]{1,0:T(8,128)(2,1)} %w_out_ref.1) | copy-start | bytes 3145732
  73.9 177.9 %all-gather.2.cloned.1.call-start = ((), (), s32[]{:S(2)}) async-start(), calls=%async_computation.2 | async-start | bytes 13369344 | tf_op jit(solution)/shard_map/all_gather | solution.py:628
  75.2 4.4 %copy-start.14 = (bf16[1024,1536]{1,0:T(8,128)(2,1)S(1)}, bf16[1024,1536]{1,0:T(8,128)(2,1)}, u32[]{:S(2)}) copy-start(bf16[1024,1536]{1,0:T(8,128)(2,1)} %w_qkv_ref.1) | copy-start | bytes 9437188
  78.9 4.3 %copy-start.41 = (bf16[64,896]{1,0:T(8,128)(2,1)}, bf16[64,896]{1,0:T(8,128)(2,1)S(1)}, u32[]{:S(2)}) copy-start(bf16[64,896]{1,0:T(8,128)(2,1)S(1)} %get-tuple-element.131.query_mark_ref) | copy-start | bytes 344068
  79.7 3.5 %copy-start.43 = (f32[128,1]{1,0:T(8,128)S(1)}, f32[128,1]{1,0:T(8,128)}, u32[]{:S(2)}) copy-start(f32[128,1]{1,0:T(8,128)} %reshape.174.gain_ref) | copy-start | bytes 1540
  83.2 12.8 %copy-start.24 = (bf16[896,1024]{1,0:T(8,128)(2,1)S(1)}, bf16[896,1024]{1,0:T(8,128)(2,1)}, u32[]{:S(2)}) copy-start(bf16[896,1024]{1,0:T(8,128)(2,1)} %get-tuple-element.84.normed_ref) | copy-start | bytes 5505028
  95.9 3.5 %copy-start.28 = (bf16[896,768]{1,0:T(8,128)(2,1)}, bf16[896,768]{1,0:T(8,128)(2,1)S(1)}, u32[]{:S(2)}) copy-start(bf16[896,768]{1,0:T(8,128)(2,1)S(1)} %get-tuple-element.82.grad_joined_ref) | copy-start | bytes 4128772
  101.8 5.6 %collective-permute-start.2 = (bf16[2,2,2,1,64,1024]{5,4,3,2,1,0:T(8,128)(2,1)}, bf16[2,2,2,1,64,1024]{5,4,3,2,1,0:T(8,128)(2,1)}, u32[]{:S(2)}, u32[]{:S(2)}) collective-permute-start(bf16[2,2,2,1,64,1024]{5,4,3,2,1,0:T(8,128)(2,1)} %constant_dynamic-slice_fusion.7), channel_id=1, source_target_pairs={{0,2},{2,0},{4,6},{6,4},{8,10},{10,8},{12,14},{14,12},{16,18},{18,... | collective-permute-start | bytes 3145736 | tf_op jit(solution)/shard_map/ppermute | solution.py:632
  103.8 3.6 %copy-start.21 = (bf16[1024,1024]{1,0:T(8,128)(2,1)S(1)}, bf16[1024,1024]{1,0:T(8,128)(2,1)}, u32[]{:S(2)}) copy-start(bf16[1024,1024]{1,0:T(8,128)(2,1)} %copy-done.20) | copy-start | bytes 6291460
  107.4 4.3 %copy-start.42 = (bf16[64,896]{1,0:T(8,128)(2,1)S(1)}, bf16[64,896]{1,0:T(8,128)(2,1)}, u32[]{:S(2)}) copy-start(bf16[64,896]{1,0:T(8,128)(2,1)} %copy-done.41) | copy-start | bytes 344068
  107.4 4.3 %copy-start.44 = (f32[128,1]{1,0:T(8,128)S(1)}, f32[128,1]{1,0:T(8,128)}, u32[]{:S(2)}) copy-start(f32[128,1]{1,0:T(8,128)} %reshape.174.gain_ref) | copy-start | bytes 1540
  110.3 14.1 %copy-start.25 = (bf16[896,1024]{1,0:T(8,128)(2,1)S(1)}, bf16[896,1024]{1,0:T(8,128)(2,1)}, u32[]{:S(2)}) copy-start(bf16[896,1024]{1,0:T(8,128)(2,1)} %get-tuple-element.84.normed_ref) | copy-start | bytes 5505028
  110.3 22.2 %collective-permute-start.3 = (bf16[1,2,2,1,64,1024]{5,4,3,2,1,0:T(8,128)(2,1)}, bf16[1,2,2,1,64,1024]{5,4,3,2,1,0:T(8,128)(2,1)}, u32[]{:S(2)}, u32[]{:S(2)}) collective-permute-start(bf16[1,2,2,1,64,1024]{5,4,3,2,1,0:T(8,128)(2,1)} %constant_dynamic-slice_fusion.6), channel_id=1, source_target_pairs={{0,4},{2,6},{4,0},{6,2},{8,12},{10,14},{12,8},{14,10},{16,20},{18,... | collective-permute-start | bytes 1572872 | tf_op jit(solution)/shard_map/ppermute | solution.py:632
  124.4 3.5 %copy-start.29 = (bf16[896,768]{1,0:T(8,128)(2,1)}, bf16[896,768]{1,0:T(8,128)(2,1)S(1)}, u32[]{:S(2)}) copy-start(bf16[896,768]{1,0:T(8,128)(2,1)S(1)} %get-tuple-element.89.grad_joined_ref) | copy-start | bytes 4128772
  124.4 3.5 %copy-start.37 = (bf16[256,896]{1,0:T(8,128)(2,1)}, bf16[256,896]{1,0:T(8,128)(2,1)S(1)}, u32[]{:S(2)}) copy-start(bf16[256,896]{1,0:T(8,128)(2,1)S(1)} %get-tuple-element.90.attended_ref) | copy-start | bytes 1376260
  130.3 12.2 %collective-permute-start.4 = (bf16[2,2,2,1,64,1024]{5,4,3,2,1,0:T(8,128)(2,1)}, bf16[2,2,2,1,64,1024]{5,4,3,2,1,0:T(8,128)(2,1)}, u32[]{:S(2)}, u32[]{:S(2)}) collective-permute-start(bf16[2,2,2,1,64,1024]{5,4,3,2,1,0:T(8,128)(2,1)} %constant_dynamic-slice_fusion.5), channel_id=1, source_target_pairs={{0,2},{2,0},{4,6},{6,4},{8,10},{10,8},{12,14},{14,12},{16,18},{18,... | collective-permute-start | bytes 3145736 | tf_op jit(solution)/shard_map/ppermute | solution.py:632
  130.5 2.1 copy-start.50
  132.3 2.5 copy-start.2
  134.9 2.1 copy-start.8
  139.0 3.5 %copy-start.19 = (bf16[1024,1024]{1,0:T(8,128)(2,1)S(1)}, bf16[1024,1024]{1,0:T(8,128)(2,1)}, u32[]{:S(2)}) copy-start(bf16[1024,1024]{1,0:T(8,128)(2,1)} %copy-done.18) | copy-start | bytes 6291460
  139.0 7.8 %copy-start.11 = (bf16[896,2048]{1,0:T(8,128)(2,1)S(1)}, bf16[896,2048]{1,0:T(8,128)(2,1)}, u32[]{:S(2)}) copy-start(bf16[896,2048]{1,0:T(8,128)(2,1)} %copy-done.10) | copy-start | bytes 11010052
  142.5 2.1 copy-start.39
  142.5 4.2 %copy-start.38 = (bf16[256,896]{1,0:T(8,128)(2,1)S(1)}, bf16[256,896]{1,0:T(8,128)(2,1)}, u32[]{:S(2)}) copy-start(bf16[256,896]{1,0:T(8,128)(2,1)} %copy-done.37) | copy-start | bytes 1376260
  142.5 4.3 %copy-start.5 = (bf16[2048,1024]{1,0:T(8,128)(2,1)S(1)}, bf16[2048,1024]{1,0:T(8,128)(2,1)}, u32[]{:S(2)}) copy-start(bf16[2048,1024]{1,0:T(8,128)(2,1)} %w_down_ref.1) | copy-start | bytes 12582916
  144.5 2.3 copy-start.32
  144.6 14.0 %collective-permute-start.7 = (bf16[1,2,2,1,64,1024]{5,4,3,2,1,0:T(8,128)(2,1)S(1)}, bf16[1,2,2,1,64,1024]{5,4,3,2,1,0:T(8,128)(2,1)S(1)}, u32[]{:S(2)}, u32[]{:S(2)}) collective-permute-start(bf16[1,2,2,1,64,1024]{5,4,3,2,1,0:T(8,128)(2,1)S(1)} %constant_dynamic-slice_fusion.2), channel_id=1, source_target_pairs={{0,4},{2,6},{4,0},{6,2},{8,12},{10,14},{12,8},{14,10},{16,20},{18,... | collective-permute-start | bytes 1572872 | tf_op jit(solution)/shard_map/ppermute | solution.py:632
  145.3 8.3 %collective-permute-start.5 = (bf16[1,2,1,1,64,1024]{5,4,3,2,1,0:T(8,128)(2,1)S(1)}, bf16[1,2,1,1,64,1024]{5,4,3,2,1,0:T(8,128)(2,1)S(1)}, u32[]{:S(2)}, u32[]{:S(2)}) collective-permute-start(bf16[1,2,1,1,64,1024]{5,4,3,2,1,0:T(8,128)(2,1)S(1)} %constant_dynamic-slice_fusion.4), channel_id=1, source_target_pairs={{0,8},{2,10},{4,12},{6,14},{8,0},{10,2},{12,4},{14,6},{16,24},{18,... | collective-permute-start | bytes 786440 | tf_op jit(solution)/shard_map/ppermute | solution.py:632
  146.8 2.6 copy-start.26
  158.8 2.5 copy-start.51
  159.6 10.7 %collective-permute-start.8 = (bf16[1,2,1,1,64,1024]{5,4,3,2,1,0:T(8,128)(2,1)}, bf16[1,2,1,1,64,1024]{5,4,3,2,1,0:T(8,128)(2,1)}, u32[]{:S(2)}, u32[]{:S(2)}) collective-permute-start(bf16[1,2,1,1,64,1024]{5,4,3,2,1,0:T(8,128)(2,1)} %constant_dynamic-slice_fusion.1), channel_id=1, source_target_pairs={{0,8},{2,10},{4,12},{6,14},{8,0},{10,2},{12,4},{14,6},{16,24},{18,... | collective-permute-start | bytes 786440 | tf_op jit(solution)/shard_map/ppermute | solution.py:632
  161.3 8.1 %collective-permute-start.6 = (bf16[1,1,1,1,64,1024]{5,4,3,2,1,0:T(8,128)(2,1)S(1)}, bf16[1,1,1,1,64,1024]{5,4,3,2,1,0:T(8,128)(2,1)S(1)}, u32[]{:S(2)}, u32[]{:S(2)}) collective-permute-start(bf16[1,1,1,1,64,1024]{5,4,3,2,1,0:T(8,128)(2,1)S(1)} %constant_dynamic-slice_fusion.3), channel_id=1, source_target_pairs={{0,16},{2,18},{4,20},{6,22},{8,24},{10,26},{12,28},{14,30},{16,0},... | collective-permute-start | bytes 393224 | tf_op jit(solution)/shard_map/ppermute | solution.py:632
  171.4 32.9 %copy-start.45 = (f32[1024]{0:T(1024)S(1)}, f32[1024]{0:T(1024)}, u32[]{:S(2)}) copy-start(f32[1024]{0:T(1024)} %param.15) | copy-start | bytes 12292
  171.4 8.7 %collective-permute-start.9 = (bf16[1,1,1,1,64,1024]{5,4,3,2,1,0:T(8,128)(2,1)S(1)}, bf16[1,1,1,1,64,1024]{5,4,3,2,1,0:T(8,128)(2,1)S(1)}, u32[]{:S(2)}, u32[]{:S(2)}) collective-permute-start(bf16[1,1,1,1,64,1024]{5,4,3,2,1,0:T(8,128)(2,1)S(1)} %constant_dynamic-slice_fusion), channel_id=1, source_target_pairs={{0,16},{2,18},{4,20},{6,22},{8,24},{10,26},{12,28},{14,30},{16,0},... | collective-permute-start | bytes 393224 | tf_op jit(solution)/shard_map/ppermute | solution.py:632
  182.2 22.0 %collective-permute-start.10 = (bf16[896,512]{1,0:T(8,128)(2,1)}, bf16[896,512]{1,0:T(8,128)(2,1)S(1)}, u32[]{:S(2)}, u32[]{:S(2)}) collective-permute-start(bf16[896,512]{1,0:T(8,128)(2,1)} %copy-done.39), channel_id=1, source_target_pairs={{0,1},{1,0},{2,3},{3,2},{4,5},{5,4},{6,7},{7,6},{8,9},{9,8},{10,11... | collective-permute-start | bytes 2752520 | tf_op jit(solution)/shard_map/ppermute | solution.py:25
  183.9 18.9 %collective-permute-start.13 = (f32[128]{0:T(128)S(1)}, f32[128]{0:T(128)S(1)}, u32[]{:S(2)}, u32[]{:S(2)}) collective-permute-start(f32[128]{0:T(128)S(1)} %add_reduce_fusion), channel_id=1, source_target_pairs={{0,1},{1,0},{2,3},{3,2},{4,5},{5,4},{6,7},{7,6},{8,9},{9,8},{10,11... | collective-permute-start | bytes 1544 | tf_op jit(solution)/shard_map/ppermute | solution.py:25
  202.8 25.9 %collective-permute-start.11 = (bf16[896,512]{1,0:T(8,128)(2,1)}, bf16[896,512]{1,0:T(8,128)(2,1)S(1)}, u32[]{:S(2)}, u32[]{:S(2)}) collective-permute-start(bf16[896,512]{1,0:T(8,128)(2,1)} %copy-done.40), channel_id=1, source_target_pairs={{0,1},{1,0},{2,3},{3,2},{4,5},{5,4},{6,7},{7,6},{8,9},{9,8},{10,11... | collective-permute-start | bytes 2752520 | tf_op jit(solution)/shard_map/ppermute | solution.py:25
  204.3 2.2 copy-start.3
  206.5 2.1 copy-start.9
  209.7 2.0 copy-start.17
  212.8 15.9 %copy-start.6 = (bf16[2048,1024]{1,0:T(8,128)(2,1)S(1)}, bf16[2048,1024]{1,0:T(8,128)(2,1)}, u32[]{:S(2)}) copy-start(bf16[2048,1024]{1,0:T(8,128)(2,1)} %w_down_ref.1) | copy-start | bytes 12582916
  212.8 15.9 %copy-start.12 = (bf16[896,2048]{1,0:T(8,128)(2,1)S(1)}, bf16[896,2048]{1,0:T(8,128)(2,1)}, u32[]{:S(2)}) copy-start(bf16[896,2048]{1,0:T(8,128)(2,1)} %copy-done.10) | copy-start | bytes 11010052
  212.8 15.9 %copy-start.27 = (bf16[512,896]{1,0:T(8,128)(2,1)S(1)}, bf16[512,896]{1,0:T(8,128)(2,1)}, u32[]{:S(2)}) copy-start(bf16[512,896]{1,0:T(8,128)(2,1)} %copy-done.26) | copy-start | bytes 2752516
  212.8 15.9 %copy-start.33 = (bf16[512,1024]{1,0:T(8,128)(2,1)S(1)}, bf16[512,1024]{1,0:T(8,128)(2,1)}, u32[]{:S(2)}) copy-start(bf16[512,1024]{1,0:T(8,128)(2,1)} %w_out_ref.1) | copy-start | bytes 3145732
  212.8 15.9 %copy-start.46 = (f32[512]{0:T(512)S(1)}, f32[512]{0:T(512)}, u32[]{:S(2)}) copy-start(f32[512]{0:T(512)} %param.22) | copy-start | bytes 6148
  216.6 15.7 %copy-start.34 = (f32[896,128]{1,0:T(8,128)}, f32[896,128]{1,0:T(8,128)S(1)}, u32[]{:S(2)}) copy-start(f32[896,128]{1,0:T(8,128)S(1)} %get-tuple-element.118.sums_ref) | copy-start | bytes 1376260
  216.7 15.7 %copy-start.36 = (f32[896,512]{1,0:T(8,128)}, f32[896,512]{1,0:T(8,128)S(1)}, u32[]{:S(2)}) copy-start(f32[896,512]{1,0:T(8,128)S(1)} %get-tuple-element.112.hat_ref) | copy-start | bytes 5505028
  216.7 1.2 collective-permute-start.14
  217.9 4.1 %collective-permute-start.15 = (f32[3200]{0:T(1024)S(1)}, f32[3200]{0:T(1024)S(1)}, u32[]{:S(2)}, u32[]{:S(2)}) collective-permute-start(f32[3200]{0:T(1024)S(1)} %fusion.9), channel_id=1, source_target_pairs={{0,4},{2,6},{4,0},{6,2},{8,12},{10,14},{12,8},{14,10},{16,20},{18,... | collective-permute-start | bytes 38408 | tf_op jit(solution)/shard_map/ppermute | solution.py:632
  222.1 4.1 %collective-permute-start.16 = (f32[3200]{0:T(1024)S(1)}, f32[3200]{0:T(1024)S(1)}, u32[]{:S(2)}, u32[]{:S(2)}) collective-permute-start(f32[3200]{0:T(1024)S(1)} %add.182), channel_id=1, source_target_pairs={{0,8},{2,10},{4,12},{6,14},{8,0},{10,2},{12,4},{14,6},{16,24},{18,... | collective-permute-start | bytes 38408 | tf_op jit(solution)/shard_map/ppermute | solution.py:632
  222.9 11.6 %collective-permute-start.12 = (f32[2,896]{0,1:T(8,128)S(1)}, f32[2,896]{0,1:T(8,128)S(1)}, u32[]{:S(2)}, u32[]{:S(2)}) collective-permute-start(f32[2,896]{0,1:T(8,128)S(1)} %slice_bitcast_fusion), channel_id=1, source_target_pairs={{0,1},{1,0},{2,3},{3,2},{4,5},{5,4},{6,7},{7,6},{8,9},{9,8},{10,11... | collective-permute-start | bytes 21512 | tf_op jit(solution)/shard_map/ppermute | solution.py:25
  226.1 13.7 %collective-permute-start.17 = (f32[3200]{0:T(1024)S(1)}, f32[3200]{0:T(1024)S(1)}, u32[]{:S(2)}, u32[]{:S(2)}) collective-permute-start(f32[3200]{0:T(1024)S(1)} %add.183), channel_id=1, source_target_pairs={{0,16},{2,18},{4,20},{6,22},{8,24},{10,26},{12,28},{14,30},{16,0},... | collective-permute-start | bytes 38408 | tf_op jit(solution)/shard_map/ppermute | solution.py:632
  251.8 4.6 %copy-start = (bf16[6144,1024]{1,0:T(8,128)(2,1)S(1)}, bf16[6144,1024]{1,0:T(8,128)(2,1)}, u32[]{:S(2)}) copy-start(bf16[6144,1024]{1,0:T(8,128)(2,1)} %all-gather.2.cloned.1.call-done) | copy-start | bytes 37748740
  (16 other events, 21.3 us)
Sparse Core Ops, SparseCore 0:
  74.0 68.7 reduce-scatter.1
  182.4 69.3 all-gather.1
